TPU v7x, 32 devices: a whole 2x2x4 slice. The times are simulated.
32 devices in a mesh: row: 4 (over y, x), col: 8 (over z, core).
Axes of the slice: x: 2, y: 2, z: 4, core: 2. Of those that a mesh axis runs over, the one named last changes fastest.
Arguments:
- transmission: float32 [2, 2, 512, 1024], P(None, None, 'row', 'col'), may hold values from -6 to 6
- probe: float32 [2, 256, 256], replicated, may hold values from -6 to 6
- fresnel_phase: float32 [256, 256], replicated, may hold values from -3.140625 to 3.140625
- amplitudes: float32 [4, 8, 1, 256, 256], P('row', 'col'), may hold values from 0.3 to 4
- positions: int32 [4, 8, 1, 2], P('row', 'col'), may hold values from 0 to 72, as said below
- tv_weight: float32 [512, 1024], P('row', 'col'), may hold values from 0.3 to 3
Outputs:
- refined: float32 [2, 2, 512, 1024], P(None, None, 'row', 'col')
Inputs may be any that keep to these rules, and one draw needn't show every extreme that they name: `positions`: over all tiles and views together, for each of the two coordinates, some view has offset 0 and some view has offset 2 * 36; a view covers rows and columns [offset, offset + 256) of its tile's region.
All inputs are finite; a program needn't handle non-finite values.
Results may differ from a plain program's by a relative error of at most 0.00016.
Values sent between devices are 32-bit elements; how exact they have to be, the bound alone decides.
A program may use at most 64 MiB of HBM per device.

v0:
```python
import functools
import math

import jax
import jax.numpy as jnp
import numpy as np
from jax import lax
from jax.experimental import pallas as pl
from jax.experimental.pallas import tpu as pltpu
from jax.sharding import PartitionSpec as P

MESH = pl.DeviceIdType.MESH
F32, BF16 = jnp.float32, jnp.bfloat16
CORE = 128
PROBE = 256
HALF = 128
BAND = 104
ROWS = BAND + CORE + BAND
COLS = 3 * CORE
HALO = 100
REACH = 3
TVROWS = 136
UPROWS = 112
AMP_EPS = 0.1
LEARN_RATE = 0.2
TV_EPS = 1.0
TV_TAU = 0.1
TV_STEPS = 3


def tables():
    k, j = np.arange(HALF)[:, None], np.arange(HALF)[None, :]
    parts = []
    for odd in (0, 1):
        angle = 2.0 * np.pi * (((2 * k + odd) * j) % PROBE) / PROBE
        c, s = np.cos(angle) / math.sqrt(PROBE), np.sin(angle) / math.sqrt(PROBE)
        full = np.block([[c, s], [-s, c]])
        parts.append(full)
    out = []
    for full in (parts[0], parts[0].T, parts[1], parts[1].T):
        full = full.astype(np.float32)
        high = full.astype(BF16)
        out += [high, (full - high.astype(np.float32)).astype(BF16)]
    order = np.zeros((PROBE, PROBE), np.float32)
    order[np.arange(HALF), 2 * np.arange(HALF)] = 1
    order[HALF + np.arange(HALF), 2 * np.arange(HALF) + 1] = 1
    out += [order.astype(BF16), order.T.astype(BF16)]
    return np.stack(out)


def split(x):
    high = x.astype(BF16)
    return high, (x - high.astype(F32)).astype(BF16)


def mm(a, b):
    return jnp.dot(a, b, preferred_element_type=F32)


def left(tab, i, x):
    wh, wl = tab[2 * i], tab[2 * i + 1]
    xh, xl = split(x)
    return mm(wh, xh) + (mm(wh, xl) + mm(wl, xh))


def right(tab, i, x):
    wh, wl = tab[2 * i], tab[2 * i + 1]
    xh, xl = split(x)
    return mm(xh, wh) + (mm(xl, wh) + mm(xh, wl))


def cat(a, b, axis):
    return jnp.concatenate([a, b], axis=axis)


def forward(tab, re, im):
    h = HALF
    e = left(tab, 0, cat(re[:h] + re[h:], im[:h] + im[h:], 0))
    o = left(tab, 2, cat(re[:h] - re[h:], im[:h] - im[h:], 0))
    re, im = cat(e[:h], o[:h], 0), cat(e[h:], o[h:], 0)
    e = right(tab, 1, cat(re[:, :h] + re[:, h:], im[:, :h] + im[:, h:], 1))
    o = right(tab, 3, cat(re[:, :h] - re[:, h:], im[:, :h] - im[:, h:], 1))
    return cat(e[:, :h], o[:, :h], 1), cat(e[:, h:], o[:, h:], 1)


def inverse(tab, re, im):
    h = HALF
    e = left(tab, 1, cat(re[:h], im[:h], 0))
    o = left(tab, 3, cat(re[h:], im[h:], 0))
    s, d = e + o, e - o
    re, im = cat(s[:h], d[:h], 0), cat(s[h:], d[h:], 0)
    e = right(tab, 0, cat(re[:, :h], im[:, :h], 1))
    o = right(tab, 2, cat(re[:, h:], im[:, h:], 1))
    s, d = e + o, e - o
    return cat(s[:, :h], d[:, :h], 1), cat(s[:, h:], d[:, h:], 1)


def reorder(tab, x):
    for axis in (0, 1):
        total = None
        rest = x
        for _ in range(3):
            part = rest.astype(BF16)
            rest = rest - part.astype(F32)
            term = mm(tab[8], part) if axis == 0 else mm(part, tab[9])
            total = term if total is None else total + term
        x = total
    return x


class Place:
    def __init__(self):
        self.r, self.c = lax.axis_index("row"), lax.axis_index("col")
        nr, nc = lax.axis_size("row"), lax.axis_size("col")
        self.has = {"up": self.r > 0, "down": self.r < nr - 1, "left": self.c > 0, "right": self.c < nc - 1}
        self.to = {"up": {"row": self.r - 1}, "down": {"row": self.r + 1}, "left": {"col": self.c - 1}, "right": {"col": self.c + 1}}

    def barrier(self):
        sem = pltpu.get_barrier_semaphore()
        for side in OPPOSITE:
            @pl.when(self.has[side])
            def _():
                pl.semaphore_signal(sem, inc=1, device_id=self.to[side], device_id_type=MESH)
        pl.semaphore_wait(sem, sum(self.has[side].astype(jnp.int32) for side in OPPOSITE))


OPPOSITE = {"up": "down", "down": "up", "left": "right", "right": "left"}


class Copy:
    def __init__(self, place, side, src, dst, sems, i, also=None):
        self.op = pltpu.make_async_remote_copy(
            src_ref=src, dst_ref=dst, send_sem=sems[0].at[i], recv_sem=sems[1].at[i],
            device_id=place.to[side], device_id_type=MESH,
        )
        self.sends, self.gets = place.has[side], place.has[OPPOSITE[side]]
        if also is not None:
            self.sends, self.gets = self.sends & also, self.gets & also

    def start(self):
        pl.when(self.sends)(lambda: self.op.start())

    def got(self):
        pl.when(self.gets)(lambda: self.op.wait_recv())

    def sent(self):
        pl.when(self.sends)(lambda: self.op.wait_send())


def whole_kernel(
    pos, tr, w, probe_any, phase_any, amp_any, tab_any, out,
    probe, phase_ref, amp, tab, ext, wext, own, lband, from_left, from_right,
    total, pack, from_up, from_down, pack_up, pack_down, send, recv, local,
):
    place = Place()
    has = place.has
    sems = (send, recv)
    loads = []
    for n, (src, dst) in enumerate(((phase_any, phase_ref), (amp_any, amp), (tab_any, tab), (probe_any, probe))):
        load = pltpu.make_async_copy(src, dst, local.at[n])
        load.start()
        loads.append(load)
    place.barrier()
    mid = pl.ds(CORE, CORE)
    lanes = {"left": pl.ds(2 * CORE, CORE), "right": pl.ds(0, CORE)}
    jobs = [(BAND, tr.at[ch], ext.at[ch]) for ch in range(4)] + [(8, w, wext)]
    copies, corners = [], []
    for ch, (band, src, dst) in enumerate(jobs):
        base = 8 * ch
        top, low = pl.ds(0, band), pl.ds(band + CORE, band)
        group = [
            Copy(place, "up", src.at[pl.ds(0, band)], dst.at[low, mid], sems, base),
            Copy(place, "down", src.at[pl.ds(CORE - band, band)], dst.at[top, mid], sems, base + 1),
            Copy(place, "left", src, dst.at[pl.ds(band, CORE), lanes["left"]], sems, base + 2),
            Copy(place, "right", src, dst.at[pl.ds(band, CORE), lanes["right"]], sems, base + 3),
        ]
        for c in group:
            c.start()
        copies.append(group)
        corner = []
        for n, (rows, there) in enumerate(((low, has["down"]), (top, has["up"]))):
            for m, side in enumerate(("left", "right")):
                corner.append(Copy(place, side, dst.at[rows, mid], dst.at[rows, lanes[side]], sems, base + 4 + 2 * n + m, there))
        corners.append(corner)

    def forward_corners(channels):
        for ch in channels:
            for n in (0, 1):
                copies[ch][n].got()
                for m in (0, 1):
                    corners[ch][2 * n + m].start()

    def arrived(channels):
        for ch in channels:
            for c in copies[ch][2:] + corners[ch]:
                c.got()

    for (band, src, dst) in jobs:
        dst[band : band + CORE, CORE : 2 * CORE] = src[...]
        rows = dst.shape[0]

        @pl.when(jnp.logical_not(has["up"]))
        def _():
            dst[0:band, :] = jnp.zeros((band, COLS), F32)

        @pl.when(jnp.logical_not(has["down"]))
        def _():
            dst[band + CORE : rows, :] = jnp.zeros((band, COLS), F32)

        @pl.when(jnp.logical_not(has["left"]))
        def _():
            dst[:, 0:CORE] = jnp.zeros((rows, CORE), F32)

        @pl.when(jnp.logical_not(has["right"]))
        def _():
            dst[:, 2 * CORE :] = jnp.zeros((rows, CORE), F32)
    edges = (
        ("left", from_left), ("right", from_right), ("up", from_up), ("down", from_down),
        ("up", pack_up), ("down", pack_down),
    )
    for side, ref in edges:
        @pl.when(jnp.logical_not(has[side]))
        def _():
            ref[...] = jnp.zeros(ref.shape, F32)

    p, q = pos[0], pos[1]

    def window(ch):
        rows = pltpu.roll(ext[ch], ROWS - (BAND - HALO) - p, 0)[:PROBE]
        return pltpu.roll(rows, COLS - (q + (CORE - HALO)), 1)[:, :PROBE]

    across = {}

    def put(ch, grad):
        wide = cat(grad, jnp.zeros((PROBE, COLS - PROBE), F32), 1)
        at_own = lax.rem(q + (COLS - HALO + REACH), COLS)
        below = jnp.zeros((ROWS - PROBE, PROBE), F32)
        down_by = p + (BAND + REACH - HALO)
        own[ch] = pltpu.roll(cat(pltpu.roll(wide, at_own, 1)[:, :PROBE], below, 0), down_by, 0)
        turned = pltpu.roll(wide, q + (CORE - REACH - HALO), 1)[:, :CORE]
        lband[ch] = pltpu.roll(cat(turned, below[:, :CORE], 0), down_by, 0)
        across[ch] = (
            Copy(place, "right", own.at[ch, :, pl.ds(CORE, CORE)], from_left.at[ch], sems, 40 + 2 * ch),
            Copy(place, "left", lband.at[ch], from_right.at[ch], sems, 41 + 2 * ch),
        )
        for c in across[ch]:
            c.start()

    for load in loads[:3]:
        load.wait()
    phase = reorder(tab, phase_ref[...])
    kr, ki = jnp.cos(phase), jnp.sin(phase)
    measured = reorder(tab, amp[...])
    loads[3].wait()
    forward_corners((0, 1))
    arrived((0, 1))
    ar, ai = window(0), window(1)
    pr, pi = probe[0], probe[1]
    fr, fi = forward(tab, ar * pr - ai * pi, ar * pi + ai * pr)
    forward_corners((2, 3))
    wr, wi = inverse(tab, kr * fr - ki * fi, kr * fi + ki * fr)
    arrived((2, 3))
    forward_corners((4,))
    br, bi = window(2), window(3)
    fr, fi = forward(tab, br * wr - bi * wi, br * wi + bi * wr)
    factor = 1.0 - measured / jnp.sqrt(fr * fr + fi * fi + AMP_EPS)
    gr, gi = inverse(tab, fr * factor, fi * factor)
    put(2, wr * gr + wi * gi)
    put(3, wr * gi - wi * gr)
    along = []
    lane = lax.broadcasted_iota(jnp.int32, (ROWS, CORE), 1)

    def fold(ch):
        for c in across[ch]:
            c.got()
        shifted = pltpu.roll(from_right[ch], 2 * REACH, 1)
        total[ch] = own[ch, :, :CORE] + from_left[ch] + jnp.where(lane >= 2 * REACH, shifted, 0.0)
        rest = jnp.where(lane < 2 * REACH, own[ch, :, CORE:] + shifted, 0.0)
        pair = (
            Copy(place, "down", total.at[ch, pl.ds(ROWS - BAND, BAND)], from_up.at[ch], sems, 48 + 2 * ch),
            Copy(place, "up", total.at[ch, pl.ds(0, UPROWS)], from_down.at[ch], sems, 49 + 2 * ch),
        )
        for c in pair:
            c.start()
        along.append(pair)
        return pltpu.roll(rest, 8 * ch, 1) if ch else rest

    fr, fi = forward(tab, br * gr + bi * gi, br * gi - bi * gr)
    gr, gi = inverse(tab, kr * fr + ki * fi, kr * fi - ki * fr)
    put(0, pr * gr + pi * gi)
    put(1, pr * gi - pi * gr)
    packed = fold(2) + fold(3) + fold(0) + fold(1)

    def compact(rows):
        rows = cat(rows, jnp.zeros((CORE - rows.shape[0], CORE), F32), 0)
        parts = [rows[32 * k : 32 * k + 32] for k in range(4)]
        return parts[0] + sum(pltpu.roll(parts[k], 32 * k, 1) for k in (1, 2, 3))

    def spread_out(x):
        return jnp.concatenate([x] + [pltpu.roll(x, CORE - 32 * k, 1) for k in (1, 2, 3)], axis=0)

    pack[0] = compact(packed[ROWS - BAND :])
    pack[1] = compact(packed[:UPROWS])
    pair = (
        Copy(place, "down", pack.at[0], pack_up, sems, 56),
        Copy(place, "up", pack.at[1], pack_down, sems, 57),
    )
    for c in pair:
        c.start()
    along.append(pair)

    arrived((4,))
    shape = (TVROWS, PROBE)
    row_at = lax.broadcasted_iota(jnp.int32, shape, 0) - REACH + place.r * CORE
    col_at = lax.broadcasted_iota(jnp.int32, shape, 1) - REACH + place.c * CORE
    inside = (row_at >= 0) & (row_at < lax.axis_size("row") * CORE) & (col_at >= 0) & (col_at < lax.axis_size("col") * CORE)
    inside = inside.astype(F32)

    def cut(ref_rows):
        return pltpu.roll(ref_rows, COLS - (CORE - REACH), 1)[:, :PROBE]

    weight = cut(wext[8 - REACH : 8 - REACH + TVROWS, :]) * inside
    for pair in along:
        for c in pair:
            c.got()

    def joined(mine, upper, lower):
        upper = cat(upper, jnp.zeros((TVROWS - BAND, CORE), F32), 0)
        lower = cat(jnp.zeros((TVROWS - UPROWS, CORE), F32), lower, 0)
        return mine[BAND : BAND + TVROWS] + upper + lower

    side = joined(packed, spread_out(pack_up[...])[:BAND], spread_out(pack_down[...])[:UPROWS])
    fields = []
    for ch in range(4):
        grad = joined(total[ch], from_up[ch], from_down[ch])
        rest = pltpu.roll(side, CORE - 8 * ch, 1) if ch else side
        field = cut(ext[ch, BAND - REACH : BAND - REACH + TVROWS, :])
        fields.append((field - LEARN_RATE * cat(grad, rest, 1)) * inside)
    for s in range(2):
        pair = fields[2 * s : 2 * s + 2]
        for _ in range(TV_STEPS):
            down = [pltpu.roll(f, TVROWS - 1, 0) - f for f in pair]
            along_row = [pltpu.roll(f, PROBE - 1, 1) - f for f in pair]
            square = down[0] * down[0] + along_row[0] * along_row[0] + (down[1] * down[1] + along_row[1] * along_row[1])
            gain = weight / jnp.sqrt(square + TV_EPS)
            fresh = []
            for f, d, r in zip(pair, down, along_row):
                d, r = gain * d, gain * r
                update = d - pltpu.roll(d, 1, 0) + (r - pltpu.roll(r, 1, 1))
                fresh.append((f + TV_TAU * update) * inside)
            pair = fresh
        for c in range(2):
            out[2 * s + c] = pltpu.roll(pair[c], PROBE - REACH, 1)[REACH : REACH + CORE, :CORE]
    for group in copies + corners + [across[ch] for ch in range(4)] + along:
        for c in group:
            c.sent()


def body(transmission, probe, fresnel_phase, amplitudes, positions, tv_weight):
    vmem, anywhere = (pl.BlockSpec(memory_space=m) for m in (pltpu.VMEM, pl.ANY))
    tab = tables()
    out = pl.pallas_call(
        whole_kernel,
        out_shape=jax.ShapeDtypeStruct((4, CORE, CORE), F32),
        in_specs=[pl.BlockSpec(memory_space=pltpu.SMEM), vmem, vmem] + [anywhere] * 4,
        out_specs=vmem,
        scratch_shapes=[
            pltpu.VMEM((2, PROBE, PROBE), F32),
            pltpu.VMEM((PROBE, PROBE), F32),
            pltpu.VMEM((PROBE, PROBE), F32),
            pltpu.VMEM(tab.shape, BF16),
            pltpu.VMEM((4, ROWS, COLS), F32),
            pltpu.VMEM((CORE + 16, COLS), F32),
            pltpu.VMEM((4, ROWS, PROBE), F32),
            pltpu.VMEM((4, ROWS, CORE), F32),
            pltpu.VMEM((4, ROWS, CORE), F32),
            pltpu.VMEM((4, ROWS, CORE), F32),
            pltpu.VMEM((4, ROWS, CORE), F32),
            pltpu.VMEM((2, 32, CORE), F32),
            pltpu.VMEM((4, BAND, CORE), F32),
            pltpu.VMEM((4, UPROWS, CORE), F32),
            pltpu.VMEM((32, CORE), F32),
            pltpu.VMEM((32, CORE), F32),
            pltpu.SemaphoreType.DMA((58,)),
            pltpu.SemaphoreType.DMA((58,)),
            pltpu.SemaphoreType.DMA((4,)),
        ],
        compiler_params=pltpu.CompilerParams(collective_id=0, has_side_effects=True),
        name="ptycho",
    )(
        positions.reshape(2), transmission.reshape(4, CORE, CORE), tv_weight, probe, fresnel_phase,
        amplitudes.reshape(PROBE, PROBE), jnp.asarray(tab),
    )
    return out.reshape(2, 2, CORE, CORE)


def solution(mesh):
    placed = (
        P(None, None, "row", "col"),
        P(),
        P(),
        P("row", "col", None, None, None),
        P("row", "col", None, None),
        P("row", "col"),
    )
    return jax.shard_map(
        body, mesh=mesh, in_specs=placed, out_specs=P(None, None, "row", "col"), check_vma=False
    )
```

profile of v0, /device:TPU:19, one launch (start us, length us, event | category | flops | bytes accessed | tf_op | source)
XLA Modules:
  0.0 43.3 jit_solution(12702513729109584769)
XLA Ops:
  0.0 41.6 %ptycho.1 = f32[4,128,128]{2,1,0:T(8,128)} custom-call(s32[2]{0:T(128)} %bitcast.7, f32[4,128,128]{2,1,0:T(8,128)} %bitcast.5, f32[128,128]{1,0:T(8,128)} %w.1, f32[2,256,256]{2,1,0:T(8,128)} %probe_any.1, f32[256,256]{1,0:T(8,128)} %phase_any.1, f32[256,256]{1,0:T(8,128)} %bitcast.6, bf16[10,256,256]{2,1,0:T(8,128)(2,1)} %constant.2.clone.tab_any), custom_call_target="tpu_custom_call" | custom-call | tf_op jit(solution)/shard_map/ptycho/pallas_call | solution.py:362
  41.6 1.7 %copy.9 = f32[2,2,128,128]{3,2,1,0:T(8,128)} copy(f32[2,2,128,128]{3,2,1,0:T(8,128)} %bitcast.4) | data formatting | bytes 524288
where the time goes:
time: 43.5 us; the launch traced here: 43.3 us
  Pallas kernels  41.6 us (96%)
  local copies, waits for them, and re-layouts  1.67 us (4%)
    pallas_call x1, Pallas kernels, body(): pl.pallas_call(whole_kernel, out_shape=jax.ShapeDtypeStruct((4, CORE, COR...  41.6 us
    unnamed x1, local copies, waits for them, and re-layouts  1.67 us

commit v1 on v0

v1 whole, which is shorter than its diff:
```python
import functools
import math

import jax
import jax.numpy as jnp
import numpy as np
from jax import lax
from jax.experimental import pallas as pl
from jax.experimental.pallas import tpu as pltpu
from jax.sharding import PartitionSpec as P

MESH = pl.DeviceIdType.MESH
F32, BF16 = jnp.float32, jnp.bfloat16
CORE = 128
PROBE = 256
HALF = 128
HALO = 100
NEAR = PROBE - CORE - HALO
STRIP = 104
REACH = 3
EDGE = 8
TVROWS = CORE + EDGE
FOLD = 16
AMP_EPS = 0.1
LEARN_RATE = 0.2
TV_EPS = 1.0
TV_TAU = 0.1
TV_STEPS = 3


def tables():
    k, j = np.arange(HALF)[:, None], np.arange(HALF)[None, :]
    parts = []
    for odd in (0, 1):
        angle = 2.0 * np.pi * (((2 * k + odd) * j) % PROBE) / PROBE
        c, s = np.cos(angle) / math.sqrt(PROBE), np.sin(angle) / math.sqrt(PROBE)
        full = np.block([[c, s], [-s, c]])
        parts.append(full)
    out = []
    for full in (parts[0], parts[0].T, parts[1], parts[1].T):
        full = full.astype(np.float32)
        high = full.astype(BF16)
        out += [high, (full - high.astype(np.float32)).astype(BF16)]
    order = np.zeros((PROBE, PROBE), np.float32)
    order[np.arange(HALF), 2 * np.arange(HALF)] = 1
    order[HALF + np.arange(HALF), 2 * np.arange(HALF) + 1] = 1
    out += [order.astype(BF16), order.T.astype(BF16)]
    return np.stack(out)


def split(x):
    high = x.astype(BF16)
    return high, (x - high.astype(F32)).astype(BF16)


def mm(a, b):
    return jnp.dot(a, b, preferred_element_type=F32)


def left(tab, i, x):
    wh, wl = tab[2 * i], tab[2 * i + 1]
    xh, xl = split(x)
    return mm(wh, xh) + (mm(wh, xl) + mm(wl, xh))


def right(tab, i, x):
    wh, wl = tab[2 * i], tab[2 * i + 1]
    xh, xl = split(x)
    return mm(xh, wh) + (mm(xl, wh) + mm(xh, wl))


def cat(a, b, axis):
    return jnp.concatenate([a, b], axis=axis)


def forward(tab, re, im):
    h = HALF
    e = left(tab, 0, cat(re[:h] + re[h:], im[:h] + im[h:], 0))
    o = left(tab, 2, cat(re[:h] - re[h:], im[:h] - im[h:], 0))
    re, im = cat(e[:h], o[:h], 0), cat(e[h:], o[h:], 0)
    e = right(tab, 1, cat(re[:, :h] + re[:, h:], im[:, :h] + im[:, h:], 1))
    o = right(tab, 3, cat(re[:, :h] - re[:, h:], im[:, :h] - im[:, h:], 1))
    return cat(e[:, :h], o[:, :h], 1), cat(e[:, h:], o[:, h:], 1)


def inverse(tab, re, im):
    h = HALF
    e = left(tab, 1, cat(re[:h], im[:h], 0))
    o = left(tab, 3, cat(re[h:], im[h:], 0))
    s, d = e + o, e - o
    re, im = cat(s[:h], d[:h], 0), cat(s[h:], d[h:], 0)
    e = right(tab, 0, cat(re[:, :h], im[:, :h], 1))
    o = right(tab, 2, cat(re[:, h:], im[:, h:], 1))
    s, d = e + o, e - o
    return cat(s[:, :h], d[:, :h], 1), cat(s[:, h:], d[:, h:], 1)


def reorder(tab, x):
    for axis in (0, 1):
        total = None
        rest = x
        for _ in range(3):
            part = rest.astype(BF16)
            rest = rest - part.astype(F32)
            term = mm(tab[8], part) if axis == 0 else mm(part, tab[9])
            total = term if total is None else total + term
        x = total
    return x


class Place:
    def __init__(self):
        self.r, self.c = lax.axis_index("row"), lax.axis_index("col")
        self.nr, self.nc = lax.axis_size("row"), lax.axis_size("col")
        self.odd = lax.rem(self.r, 2)
        step = 1 - 2 * self.odd
        rows = {"mate": self.r + step, "other": self.r - step, "ahead": self.r + 2 * step, "behind": self.r - 2 * step}
        self.to = {side: {"row": at} for side, at in rows.items()}
        self.has = {side: (at >= 0) & (at < self.nr) for side, at in rows.items()}
        for side, at in (("left", self.c - 1), ("right", self.c + 1)):
            self.to[side] = {"col": at}
            self.has[side] = (at >= 0) & (at < self.nc)

    def signal(self):
        sem = pltpu.get_barrier_semaphore()
        for side in OPPOSITE:
            @pl.when(self.has[side])
            def _():
                pl.semaphore_signal(sem, inc=1, device_id=self.to[side], device_id_type=MESH)

    def wait(self):
        sem = pltpu.get_barrier_semaphore()
        pl.semaphore_wait(sem, sum(self.has[side].astype(jnp.int32) for side in OPPOSITE))


OPPOSITE = {"left": "right", "right": "left", "mate": "mate", "other": "other", "ahead": "behind", "behind": "ahead"}


class Wire:
    def __init__(self, place, send, recv):
        self.place, self.send, self.recv = place, send, recv
        self.count, self.all = 0, []

    def __call__(self, side, src, dst):
        copy = Copy(self.place, side, src, dst, self.send.at[self.count], self.recv.at[self.count])
        self.count += 1
        self.all.append(copy)
        return copy


class Copy:
    def __init__(self, place, side, src, dst, send, recv):
        self.op = pltpu.make_async_remote_copy(
            src_ref=src, dst_ref=dst, send_sem=send, recv_sem=recv, device_id=place.to[side], device_id_type=MESH,
        )
        self.sends, self.gets = place.has[side], place.has[OPPOSITE[side]]

    def start(self):
        pl.when(self.sends)(lambda: self.op.start())

    def got(self):
        pl.when(self.gets)(lambda: self.op.wait_recv())

    def sent(self):
        pl.when(self.sends)(lambda: self.op.wait_send())


def iota(shape, axis):
    return lax.broadcasted_iota(jnp.int32, shape, axis)


def tall(tile):
    return cat_rows([tile] * (CORE // EDGE))


def cat_rows(parts):
    return jnp.concatenate(parts, axis=0)


def compact(x):
    parts = [x[FOLD * k : FOLD * k + FOLD] for k in range(CORE // FOLD)]
    return parts[0] + sum(pltpu.roll(part, FOLD * k, 1) for k, part in enumerate(parts) if k)


def expand(x):
    return cat_rows([x] + [pltpu.roll(x, CORE - FOLD * k, 1) for k in range(1, CORE // FOLD)])


def squeeze(x, n):
    lane = iota(x.shape, 1)
    x = jnp.where((lane < REACH) | (lane >= CORE - REACH), x, 0.0)
    return pltpu.roll(x, REACH + 8 * n, 1)


def whole_kernel(
    pos_any, tr_any, w_any, probe_any, phase_any, amp_any, tab_any, out,
    pos, tile, w, probe, phase_ref, amp, tab,
    hl, hr, cl, cr, mt, nm, outl, outr, place_me, place_l, place_r, xs,
    w_rows, w_mate, w_other, w_pack, w_left, w_right,
    g, gl, gr, il, ir, tot, edge, side_out, side_in, mate_out, mate_in,
    ptot, pedge, pmate, prim, pside_out, pside_in, pmate_out, pmate_in,
    send, recv, local,
):
    place = Place()
    has, odd = place.has, place.odd
    place.signal()
    loads = []
    pairs = (
        (tr_any, tile), (pos_any, pos), (phase_any, phase_ref), (tab_any, tab), (amp_any, amp), (probe_any, probe), (w_any, w),
    )
    for n, (src, dst) in enumerate(pairs):
        load = pltpu.make_async_copy(src, dst, local.at[n])
        load.start()
        loads.append(load)
    wire = Wire(place, send, recv)
    for side, refs in (
        ("left", (hl, cl, il, place_l, w_left)), ("right", (hr, cr, ir, place_r, w_right)),
        ("other", (nm, w_other)), ("ahead", (side_in, pside_in)),
    ):
        @pl.when(jnp.logical_not(has[side]))
        def _():
            for ref in refs:
                ref[...] = jnp.zeros(ref.shape, F32)
    loads[1].wait()
    p, q = pos[0], pos[1]
    place_me[...] = jnp.full((EDGE, CORE), p.astype(F32))
    loads[0].wait()
    place.wait()

    low_strip = pl.ds(pl.multiple_of((CORE - STRIP) * odd, EDGE), STRIP)
    high_strip = pl.ds(pl.multiple_of((CORE - STRIP) * (1 - odd), EDGE), STRIP)
    direct = {ch: wire("other", tile.at[ch, low_strip], nm.at[ch, low_strip]) for ch in DIRECT_A}
    to_mate = [wire("mate", tile.at[ch], mt.at[ch]) for ch in range(4)]
    to_left = [wire("left", tile.at[ch], hr.at[ch]) for ch in range(4)]
    to_right = [wire("right", tile.at[ch], hl.at[ch]) for ch in range(4)]
    relay = {ch: wire("ahead", mt.at[ch, high_strip], nm.at[ch, high_strip]) for ch in range(4) if ch not in direct}
    spots = [wire("left", place_me, place_r), wire("right", place_me, place_l)]
    corner_left = [wire("left", outl.at[ch], cr.at[ch]) for ch in range(4)]
    corner_right = [wire("right", outr.at[ch], cl.at[ch]) for ch in range(4)]
    w_steps = [wire("mate", w_rows, w_mate), wire("other", w_rows, w_other)]
    w_sides = [wire("left", w_pack, w_right), wire("right", w_pack, w_left)]
    for c in spots:
        c.start()
    for ch in range(4):
        if ch in direct:
            direct[ch].start()
        to_mate[ch].start()
        to_left[ch].start()
        to_right[ch].start()
    loads[6].wait()
    w_rows[0:EDGE] = w[0:EDGE]
    w_rows[EDGE:] = w[CORE - EDGE :]
    for c in w_steps:
        c.start()

    sign = (1 - 2 * odd).astype(F32)
    block = (CORE, CORE)
    row = iota(block, 0).astype(F32) - (NEAR - 0.5)
    lane = iota(block, 1)
    sub = iota((EDGE, CORE), 0)
    nearer = lane < NEAR + q
    own_rows = row < p.astype(F32)

    def is_even(shape):
        return jnp.full(shape, odd, jnp.int32) == 0

    def forward_rows(channels):
        for ch in channels:
            to_mate[ch].got()
            if ch in relay:
                relay[ch].start()

    def forward_corners(channels):
        if 0 in channels:
            for c in spots:
                c.got()
        to_l = sign * (row - tall(place_l[...])) < 0
        to_r = sign * (row - tall(place_r[...])) < 0
        for ch in channels:
            (direct[ch] if ch in direct else relay[ch]).got()
            m, n = mt[ch], nm[ch]
            outl[ch] = jnp.where(to_l, m, n)
            corner_left[ch].start()
            outr[ch] = jnp.where(to_r, m, n)
            corner_right[ch].start()

    mate_rows = sign * (row - p.astype(F32)) < 0

    def assemble(ch):
        to_left[ch].got()
        to_right[ch].got()
        h = jnp.where(nearer, hr[ch], hl[ch])
        v = jnp.where(mate_rows, mt[ch], nm[ch])
        corner_left[ch].got()
        corner_right[ch].got()
        c = jnp.where(nearer, cr[ch], cl[ch])
        xs[ch] = cat(cat(tile[ch], h, 1), cat(v, c, 1), 0)

    loads[2].wait()
    loads[3].wait()
    phase = reorder(tab, phase_ref[...])
    kr, ki = jnp.cos(phase), jnp.sin(phase)
    forward_rows((0, 1))
    loads[5].wait()
    turn_rows, turn_cols = p + (PROBE - HALO), q + (PROBE - HALO)
    pr, pi = (pltpu.roll(pltpu.roll(probe[n], turn_rows, 0), turn_cols, 1) for n in range(2))
    loads[4].wait()
    measured = reorder(tab, amp[...])
    forward_corners((0, 1))
    forward_rows((2, 3))
    assemble(0)
    assemble(1)
    ar, ai = xs[0], xs[1]
    fr, fi = forward(tab, ar * pr - ai * pi, ar * pi + ai * pr)
    forward_corners((2, 3))
    wr, wi = inverse(tab, kr * fr - ki * fi, kr * fi + ki * fr)
    assemble(2)
    assemble(3)
    br, bi = xs[2], xs[3]
    fr, fi = forward(tab, br * wr - bi * wi, br * wi + bi * wr)
    for c in w_steps:
        c.got()
    thin = is_even((EDGE, CORE))
    below = jnp.where(thin, w_mate[0:EDGE], w_other[0:EDGE])
    above = jnp.where(thin, w_other[EDGE:], w_mate[EDGE:])
    w_edge = jnp.where(sub < EDGE // 2, below, above)
    w_pack[0:FOLD] = compact(squeeze(w[...], 0))
    w_pack[FOLD:] = squeeze(w_edge, 0)
    for c in w_sides:
        c.start()
    factor = 1.0 - measured / jnp.sqrt(fr * fr + fi * fi + AMP_EPS)
    gr_, gi_ = inverse(tab, fr * factor, fi * factor)

    across = {}
    lanes = iota((PROBE, CORE), 1)
    near_lanes = lanes < NEAR + q

    def put(ch, grad):
        g[ch] = grad
        own, halo = grad[:, :CORE], grad[:, CORE:]
        across[ch] = (wire("right", gr.at[ch], il.at[ch]), wire("left", gl.at[ch], ir.at[ch]))
        gr[ch] = jnp.where(lanes >= CORE - REACH, own, jnp.where(near_lanes, halo, 0.0))
        across[ch][0].start()
        gl[ch] = jnp.where(lanes < REACH, own, jnp.where(near_lanes, 0.0, halo))
        across[ch][1].start()

    upward, onward = {}, {}

    lo, hi = CORE - STRIP, STRIP - EDGE

    def shares(t, down, up):
        even, thin = is_even(block), is_even((EDGE, CORE))
        rim = jnp.where(sub < REACH, down[:EDGE], jnp.where(sub >= EDGE - REACH, up[CORE - EDGE :], 0.0))
        first, last = t[:EDGE], t[CORE - EDGE :]
        up_far = cat_rows([up[:lo], jnp.where(sub < REACH, first, up[lo : lo + EDGE]), up[lo + EDGE :]])
        down_far = cat_rows([down[:hi], jnp.where(sub >= EDGE - REACH, last, down[hi : hi + EDGE]), down[hi + EDGE :]])
        mate_rim = jnp.where(thin, jnp.where(sub >= EDGE - REACH, last, 0.0), jnp.where(sub < REACH, first, 0.0))
        return rim, jnp.where(even, up_far, down_far), jnp.where(even, down, up), mate_rim

    def fold(s):
        in_l = row < tall(place_l[...])
        in_r = row < tall(place_r[...])
        low = lane < REACH
        in_side = jnp.where(low, row - tall(place_r[...]), row - tall(place_l[...])) < 0
        packed = [0.0, 0.0, 0.0]
        for n in range(2):
            ch = 2 * s + n
            for c in across[ch]:
                c.got()
            fl, fr = il[ch], ir[ch]
            own, halo = g[ch, :, :CORE], g[ch, :, CORE:]
            parts = (
                (own_rows, own), (in_l, jnp.where(lanes < CORE - REACH, fl, 0.0)), (in_r, jnp.where(lanes >= REACH, fr, 0.0)),
            )
            t = sum(x[:CORE] for _, x in parts)
            down = sum(jnp.where(m, x[CORE:], 0.0) for m, x in parts)
            up = sum(jnp.where(m, 0.0, x[CORE:]) for m, x in parts)
            tot[ch] = t
            edge[ch], side_out[ch], mate_out[ch, :CORE], mate_out[ch, CORE:] = shares(t, down, up)
            upward[ch] = wire("behind", side_out.at[ch, high_strip], side_in.at[ch, high_strip])
            upward[ch].start()
            h, o = halo[CORE:], jnp.where(low, fr[CORE:], fl[CORE:])
            pieces = (
                halo[:CORE] + jnp.where(low, fr[:CORE], fl[:CORE]),
                jnp.where(own_rows, h, 0.0) + jnp.where(in_side, o, 0.0),
                jnp.where(own_rows, 0.0, h) + jnp.where(in_side, 0.0, o),
            )
            packed = [a + squeeze(b, n) for a, b in zip(packed, pieces)]
        ptot[s] = packed[0]
        pedge[s], far, pmate[s], prim[s] = shares(*packed)
        pside_out[s] = compact(far)
        upward[4 + s] = wire("behind", pside_out.at[s], pside_in.at[s])
        upward[4 + s].start()

    def incoming(x):
        fill = jnp.where(is_even(block), jnp.where(row > 0, x, 0.0), jnp.where(row < HALO - NEAR, x, 0.0))
        rim = jnp.where(
            is_even((EDGE, CORE)),
            jnp.where(sub < REACH, x[lo : lo + EDGE], 0.0),
            jnp.where(sub >= EDGE - REACH, x[hi : hi + EDGE], 0.0),
        )
        return fill, rim

    def pass_on(s):
        for ch in (2 * s, 2 * s + 1):
            upward[ch].got()
            fill, rim = incoming(side_in[ch])
            mate_out[ch, :CORE] += fill
            mate_out[ch, CORE:] += rim
            onward[ch] = wire("mate", mate_out.at[ch], mate_in.at[ch])
            onward[ch].start()
        upward[4 + s].got()
        fill, rim = incoming(jnp.where(lane < FOLD, expand(pside_in[s]), 0.0))
        pmate_out[s, :FOLD] = compact(pmate[s] + fill)
        pmate_out[s, FOLD:] = prim[s] + rim
        onward[4 + s] = wire("mate", pmate_out.at[s], pmate_in.at[s])
        onward[4 + s].start()

    shape = (TVROWS, PROBE)

    def smooth(s):
        onward[4 + s].got()
        rest = cat_rows([ptot[s] + expand(pmate_in[s, :FOLD]), pedge[s] + pmate_in[s, FOLD:]])
        pair = []
        for n in range(2):
            ch = 2 * s + n
            onward[ch].got()
            grad = cat_rows([tot[ch] + mate_in[ch, :CORE], edge[ch] + mate_in[ch, CORE:]])
            grad = cat(grad, pltpu.roll(rest, CORE - REACH - 8 * n, 1), 1)
            wide = iota((EDGE, PROBE), 0) < EDGE // 2
            rim = jnp.where(wide, xs[ch, CORE : CORE + EDGE, :], xs[ch, PROBE - EDGE :, :])
            field = cat_rows([xs[ch, :CORE, :], rim])
            pair.append((field - LEARN_RATE * grad) * inside)
        for _ in range(TV_STEPS):
            down = [pltpu.roll(f, TVROWS - 1, 0) - f for f in pair]
            along_row = [pltpu.roll(f, PROBE - 1, 1) - f for f in pair]
            square = down[0] * down[0] + along_row[0] * along_row[0] + (down[1] * down[1] + along_row[1] * along_row[1])
            gain = weight / jnp.sqrt(square + TV_EPS)
            fresh = []
            for f, d, r in zip(pair, down, along_row):
                d, r = gain * d, gain * r
                update = d - pltpu.roll(d, 1, 0) + (r - pltpu.roll(r, 1, 1))
                fresh.append((f + TV_TAU * update) * inside)
            pair = fresh
        for n in range(2):
            out[2 * s + n] = pair[n][:CORE, :CORE]

    put(2, wr * gr_ + wi * gi_)
    put(3, wr * gi_ - wi * gr_)
    fr, fi = forward(tab, br * gr_ + bi * gi_, br * gi_ - bi * gr_)
    gr_, gi_ = inverse(tab, kr * fr + ki * fi, kr * fi - ki * fr)
    put(0, pr * gr_ + pi * gi_)
    put(1, pr * gi_ - pi * gr_)
    fold(1)
    for c in w_sides:
        c.got()
    row_at, col_at = iota(shape, 0), iota(shape, 1)
    row_at = place.r * CORE + jnp.where(row_at < CORE + EDGE // 2, row_at, row_at - TVROWS)
    col_at = place.c * CORE + jnp.where(col_at < CORE + HALF // 2, col_at, col_at - PROBE)
    inside = (row_at >= 0) & (row_at < place.nr * CORE) & (col_at >= 0) & (col_at < place.nc * CORE)
    inside = inside.astype(F32)
    margins = [cat_rows([expand(ref[:FOLD]), ref[FOLD:]]) for ref in (w_right, w_left)]
    margins = [pltpu.roll(m, CORE - REACH, 1) for m in margins]
    far = jnp.where(iota((TVROWS, CORE), 1) < HALF // 2, margins[0], margins[1])
    weight = cat(cat_rows([w[...], w_edge]), far, 1) * inside
    pass_on(1)
    fold(0)
    smooth(1)
    pass_on(0)
    smooth(0)
    for c in wire.all:
        c.sent()


DIRECT_A = ()


def body(transmission, probe, fresnel_phase, amplitudes, positions, tv_weight):
    vmem, anywhere = (pl.BlockSpec(memory_space=m) for m in (pltpu.VMEM, pl.ANY))
    tab = tables()

    def scratch(*shape):
        return pltpu.VMEM(shape, F32)

    four = lambda n: [scratch(4, CORE, CORE)] * n
    small = lambda n: [scratch(EDGE, CORE)] * n
    count = 48
    out = pl.pallas_call(
        whole_kernel,
        out_shape=jax.ShapeDtypeStruct((4, CORE, CORE), F32),
        in_specs=[anywhere] * 7,
        out_specs=vmem,
        scratch_shapes=[
            pltpu.SMEM((2,), jnp.int32), scratch(4, CORE, CORE), scratch(CORE, CORE), scratch(2, PROBE, PROBE),
            scratch(PROBE, PROBE), scratch(PROBE, PROBE), pltpu.VMEM(tab.shape, BF16),
            *four(8), *small(3), scratch(4, PROBE, PROBE),
            *[scratch(2 * EDGE, CORE)] * 3, *[scratch(FOLD + EDGE, CORE)] * 3,
            scratch(4, PROBE, PROBE), *[scratch(4, PROBE, CORE)] * 4,
            scratch(4, CORE, CORE), scratch(4, EDGE, CORE), *four(2), *[scratch(4, TVROWS, CORE)] * 2,
            scratch(2, CORE, CORE), scratch(2, EDGE, CORE), scratch(2, CORE, CORE), scratch(2, EDGE, CORE),
            *[scratch(2, FOLD, CORE)] * 2,
            *[scratch(2, FOLD + EDGE, CORE)] * 2,
            pltpu.SemaphoreType.DMA((count + 8,)),
            pltpu.SemaphoreType.DMA((count + 8,)),
            pltpu.SemaphoreType.DMA((7,)),
        ],
        compiler_params=pltpu.CompilerParams(collective_id=0, has_side_effects=True),
        name="ptycho",
    )(
        positions.reshape(2), transmission.reshape(4, CORE, CORE), tv_weight, probe, fresnel_phase,
        amplitudes.reshape(PROBE, PROBE), jnp.asarray(tab),
    )
    return out.reshape(2, 2, CORE, CORE)


def solution(mesh):
    placed = (
        P(None, None, "row", "col"),
        P(),
        P(),
        P("row", "col", None, None, None),
        P("row", "col", None, None),
        P("row", "col"),
    )
    return jax.shard_map(
        body, mesh=mesh, in_specs=placed, out_specs=P(None, None, "row", "col"), check_vma=False
    )
```

time: 43.5 us -> 41.5 us (0.954)
  the two profiles are of different devices: /device:TPU:19 before, /device:TPU:1 now
where the time goes in v1:
time: 41.5 us; the launch traced here: 41.3 us
  Pallas kernels  39.7 us (96%)
  local copies, waits for them, and re-layouts  1.67 us (4%)
    pallas_call x1, Pallas kernels, body(): pl.pallas_call(whole_kernel, out_shape=jax.ShapeDtypeStruct((4, CORE, COR...  39.7 us
    unnamed x1, local copies, waits for them, and re-layouts  1.67 us

profile of v1, /device:TPU:1, one launch (start us, length us, event | category | flops | bytes accessed | tf_op | source)
XLA Modules:
  0.0 41.3 jit_solution(16865298548550696467)
XLA Ops:
  0.0 39.7 %ptycho.1 = f32[4,128,128]{2,1,0:T(8,128)} custom-call(s32[2]{0:T(128)} %bitcast.7, f32[4,128,128]{2,1,0:T(8,128)} %bitcast.5, f32[128,128]{1,0:T(8,128)} %w_any.1, f32[2,256,256]{2,1,0:T(8,128)} %probe_any.1, f32[256,256]{1,0:T(8,128)} %phase_any.1, f32[256,256]{1,0:T(8,128)} %bitcast.6, bf16[10,256,256]{2,1,0:T(8,128)(2,1)} %constant.2.clone.tab_any), custom_call_target="tpu_custom_call" | custom-call | tf_op jit(solution)/shard_map/ptycho/pallas_call | solution.py:488
  39.7 1.7 %copy.9 = f32[2,2,128,128]{3,2,1,0:T(8,128)} copy(f32[2,2,128,128]{3,2,1,0:T(8,128)} %bitcast.4) | data formatting | bytes 524288

commit v2 on v1

--- a/solution.py
+++ b/solution.py
@@ -142,7 +142,7 @@
         self.count, self.all = 0, []
 
     def __call__(self, side, src, dst):
-        copy = Copy(self.place, side, src, dst, self.send.at[self.count], self.recv.at[self.count])
+        copy = Copy(self.place, side, src, dst, self.send.at[list(OPPOSITE).index(side)], self.recv.at[self.count])
         self.count += 1
         self.all.append(copy)
         return copy
@@ -197,7 +197,7 @@
     pos, tile, w, probe, phase_ref, amp, tab,
     hl, hr, cl, cr, mt, nm, outl, outr, place_me, place_l, place_r, xs,
     w_rows, w_mate, w_other, w_pack, w_left, w_right,
-    g, gl, gr, il, ir, tot, edge, side_out, side_in, mate_out, mate_in,
+    g, gl, gr, il, ir, tot, edge, side_out, side_in, near_out, near_in, mate_out, mate_in,
     ptot, pedge, pmate, prim, pside_out, pside_in, pmate_out, pmate_in,
     send, recv, local,
 ):
@@ -215,7 +215,8 @@
     wire = Wire(place, send, recv)
     for side, refs in (
         ("left", (hl, cl, il, place_l, w_left)), ("right", (hr, cr, ir, place_r, w_right)),
-        ("other", (nm, w_other)), ("ahead", (side_in, pside_in)),
+        ("other", (nm, w_other, *(side_in.at[ch] for ch in DIRECT_B))),
+        ("ahead", (pside_in, *(side_in.at[ch] for ch in range(4) if ch not in DIRECT_B))),
     ):
         @pl.when(jnp.logical_not(has[side]))
         def _():
@@ -231,8 +232,9 @@
     high_strip = pl.ds(pl.multiple_of((CORE - STRIP) * (1 - odd), EDGE), STRIP)
     direct = {ch: wire("other", tile.at[ch, low_strip], nm.at[ch, low_strip]) for ch in DIRECT_A}
     to_mate = [wire("mate", tile.at[ch], mt.at[ch]) for ch in range(4)]
-    to_left = [wire("left", tile.at[ch], hr.at[ch]) for ch in range(4)]
-    to_right = [wire("right", tile.at[ch], hl.at[ch]) for ch in range(4)]
+    slices = [pl.ds(2 * s, 2) for s in range(2)]
+    to_left = [wire("left", tile.at[part], hr.at[part]) for part in slices]
+    to_right = [wire("right", tile.at[part], hl.at[part]) for part in slices]
     relay = {ch: wire("ahead", mt.at[ch, high_strip], nm.at[ch, high_strip]) for ch in range(4) if ch not in direct}
     spots = [wire("left", place_me, place_r), wire("right", place_me, place_l)]
     corner_left = [wire("left", outl.at[ch], cr.at[ch]) for ch in range(4)]
@@ -245,8 +247,9 @@
         if ch in direct:
             direct[ch].start()
         to_mate[ch].start()
-        to_left[ch].start()
-        to_right[ch].start()
+        if ch % 2 == 0:
+            to_left[ch // 2].start()
+            to_right[ch // 2].start()
     loads[6].wait()
     w_rows[0:EDGE] = w[0:EDGE]
     w_rows[EDGE:] = w[CORE - EDGE :]
@@ -287,8 +290,9 @@
     mate_rows = sign * (row - p.astype(F32)) < 0
 
     def assemble(ch):
-        to_left[ch].got()
-        to_right[ch].got()
+        if ch % 2 == 0:
+            to_left[ch // 2].got()
+            to_right[ch // 2].got()
         h = jnp.where(nearer, hr[ch], hl[ch])
         v = jnp.where(mate_rows, mt[ch], nm[ch])
         corner_left[ch].got()
@@ -300,19 +304,23 @@
     loads[3].wait()
     phase = reorder(tab, phase_ref[...])
     kr, ki = jnp.cos(phase), jnp.sin(phase)
-    forward_rows((0, 1))
+    forward_rows((0,))
+    forward_rows((1,))
+    forward_corners((0,))
     loads[5].wait()
     turn_rows, turn_cols = p + (PROBE - HALO), q + (PROBE - HALO)
     pr, pi = (pltpu.roll(pltpu.roll(probe[n], turn_rows, 0), turn_cols, 1) for n in range(2))
+    forward_corners((1,))
+    forward_rows((2,))
     loads[4].wait()
     measured = reorder(tab, amp[...])
-    forward_corners((0, 1))
-    forward_rows((2, 3))
+    forward_rows((3,))
+    forward_corners((3,))
+    forward_corners((2,))
     assemble(0)
     assemble(1)
     ar, ai = xs[0], xs[1]
     fr, fi = forward(tab, ar * pr - ai * pi, ar * pi + ai * pr)
-    forward_corners((2, 3))
     wr, wi = inverse(tab, kr * fr - ki * fi, kr * fi + ki * fr)
     assemble(2)
     assemble(3)
@@ -334,87 +342,133 @@
     across = {}
     lanes = iota((PROBE, CORE), 1)
     near_lanes = lanes < NEAR + q
+    body_rows, rim_rows = pl.ds(0, CORE - 2 * EDGE), pl.ds(CORE - 2 * EDGE, PROBE - CORE + 2 * EDGE)
 
     def put(ch, grad):
         g[ch] = grad
         own, halo = grad[:, :CORE], grad[:, CORE:]
-        across[ch] = (wire("right", gr.at[ch], il.at[ch]), wire("left", gl.at[ch], ir.at[ch]))
-        gr[ch] = jnp.where(lanes >= CORE - REACH, own, jnp.where(near_lanes, halo, 0.0))
-        across[ch][0].start()
-        gl[ch] = jnp.where(lanes < REACH, own, jnp.where(near_lanes, 0.0, halo))
-        across[ch][1].start()
+        to_r = jnp.where(lanes >= CORE - REACH, own, jnp.where(near_lanes, halo, 0.0))
+        to_l = jnp.where(lanes < REACH, own, jnp.where(near_lanes, 0.0, halo))
+        for n, (ref, x) in enumerate(((gr, to_r), (gl, to_l))):
+            ref[ch] = cat_rows([x[EDGE:], x[:EDGE]])
+        across[ch] = cross(ch, rim_rows)
+
+    def cross(which, rows):
+        pair = wire("right", gr.at[which, rows], il.at[which, rows]), wire("left", gl.at[which, rows], ir.at[which, rows])
+        for c in pair:
+            c.start()
+        return pair
 
     upward, onward = {}, {}
 
     lo, hi = CORE - STRIP, STRIP - EDGE
 
-    def shares(t, down, up):
+    def shares(first, last, down, up):
         even, thin = is_even(block), is_even((EDGE, CORE))
         rim = jnp.where(sub < REACH, down[:EDGE], jnp.where(sub >= EDGE - REACH, up[CORE - EDGE :], 0.0))
-        first, last = t[:EDGE], t[CORE - EDGE :]
         up_far = cat_rows([up[:lo], jnp.where(sub < REACH, first, up[lo : lo + EDGE]), up[lo + EDGE :]])
         down_far = cat_rows([down[:hi], jnp.where(sub >= EDGE - REACH, last, down[hi : hi + EDGE]), down[hi + EDGE :]])
+        far, near = jnp.where(even, up_far, down_far), jnp.where(even, down_far, up_far)
         mate_rim = jnp.where(thin, jnp.where(sub >= EDGE - REACH, last, 0.0), jnp.where(sub < REACH, first, 0.0))
-        return rim, jnp.where(even, up_far, down_far), jnp.where(even, down, up), mate_rim
-
-    def fold(s):
+        return rim, far, near, jnp.where(even, down, up), mate_rim
+
+    bands = ((slice(0, EDGE), slice(PROBE - EDGE, PROBE)), (slice(CORE - EDGE, CORE), slice(CORE - 2 * EDGE, CORE - EDGE)))
+
+    def joined(ch, mine, theirs):
+        own, halo = g[ch, mine, :CORE], g[ch, mine, CORE:]
+        fl, fr = il[ch, theirs], ir[ch, theirs]
+        lane = iota(own.shape, 1)
+        total = own + jnp.where(lane < CORE - REACH, fl, 0.0) + jnp.where(lane >= REACH, fr, 0.0)
+        return total, halo + jnp.where(lane < REACH, fr, fl)
+
+    packs = {}
+
+    def fold(ch):
+        s, n = divmod(ch, 2)
+        for c in across[ch]:
+            c.got()
         in_l = row < tall(place_l[...])
         in_r = row < tall(place_r[...])
         low = lane < REACH
         in_side = jnp.where(low, row - tall(place_r[...]), row - tall(place_l[...])) < 0
-        packed = [0.0, 0.0, 0.0]
-        for n in range(2):
-            ch = 2 * s + n
-            for c in across[ch]:
-                c.got()
-            fl, fr = il[ch], ir[ch]
-            own, halo = g[ch, :, :CORE], g[ch, :, CORE:]
-            parts = (
-                (own_rows, own), (in_l, jnp.where(lanes < CORE - REACH, fl, 0.0)), (in_r, jnp.where(lanes >= REACH, fr, 0.0)),
-            )
-            t = sum(x[:CORE] for _, x in parts)
-            down = sum(jnp.where(m, x[CORE:], 0.0) for m, x in parts)
-            up = sum(jnp.where(m, 0.0, x[CORE:]) for m, x in parts)
-            tot[ch] = t
-            edge[ch], side_out[ch], mate_out[ch, :CORE], mate_out[ch, CORE:] = shares(t, down, up)
+        far_rows = slice(CORE - EDGE, PROBE - EDGE)
+        own, halo, fl, fr = g[ch, CORE:, :CORE], g[ch, CORE:, CORE:], il[ch, far_rows], ir[ch, far_rows]
+        parts = ((own_rows, own), (in_l, jnp.where(lane < CORE - REACH, fl, 0.0)), (in_r, jnp.where(lane >= REACH, fr, 0.0)))
+        down = sum(jnp.where(m, x, 0.0) for m, x in parts)
+        up = sum(jnp.where(m, 0.0, x) for m, x in parts)
+        ends = [joined(ch, *band) for band in bands]
+        rim, far, near, base, mate_rim = shares(ends[0][0], ends[1][0], down, up)
+        edge[ch], side_out[ch] = rim, far
+        if ch in DIRECT_B:
+            near_out[ch] = near
+            upward[ch] = wire("other", side_out.at[ch, high_strip], side_in.at[ch, high_strip])
+            onward[ch] = wire("mate", near_out.at[ch, low_strip], near_in.at[ch, low_strip])
+            upward[ch].start()
+            onward[ch].start()
+        else:
             upward[ch] = wire("behind", side_out.at[ch, high_strip], side_in.at[ch, high_strip])
             upward[ch].start()
-            h, o = halo[CORE:], jnp.where(low, fr[CORE:], fl[CORE:])
-            pieces = (
-                halo[:CORE] + jnp.where(low, fr[:CORE], fl[:CORE]),
-                jnp.where(own_rows, h, 0.0) + jnp.where(in_side, o, 0.0),
-                jnp.where(own_rows, 0.0, h) + jnp.where(in_side, 0.0, o),
-            )
-            packed = [a + squeeze(b, n) for a, b in zip(packed, pieces)]
-        ptot[s] = packed[0]
-        pedge[s], far, pmate[s], prim[s] = shares(*packed)
+            mate_out[ch, :CORE], mate_out[ch, CORE:] = base, mate_rim
+        o = jnp.where(low, fr, fl)
+        pieces = [
+            ends[0][1], ends[1][1],
+            jnp.where(own_rows, halo, 0.0) + jnp.where(in_side, o, 0.0),
+            jnp.where(own_rows, 0.0, halo) + jnp.where(in_side, 0.0, o),
+        ]
+        pieces = [squeeze(x, n) for x in pieces]
+        if n == 0:
+            packs[s] = pieces
+            return
+        pedge[s], far, _, pmate[s], prim[s] = shares(*[a + b for a, b in zip(packs[s], pieces)])
         pside_out[s] = compact(far)
         upward[4 + s] = wire("behind", pside_out.at[s], pside_in.at[s])
         upward[4 + s].start()
 
-    def incoming(x):
-        fill = jnp.where(is_even(block), jnp.where(row > 0, x, 0.0), jnp.where(row < HALO - NEAR, x, 0.0))
-        rim = jnp.where(
-            is_even((EDGE, CORE)),
-            jnp.where(sub < REACH, x[lo : lo + EDGE], 0.0),
-            jnp.where(sub >= EDGE - REACH, x[hi : hi + EDGE], 0.0),
-        )
-        return fill, rim
-
-    def pass_on(s):
-        for ch in (2 * s, 2 * s + 1):
+    def fill(s):
+        for c in inner[s]:
+            c.got()
+        for n in range(2):
+            ch = 2 * s + n
+            parts = [joined(ch, *bands[0])]
+            parts.append(joined(ch, slice(EDGE, CORE - EDGE), slice(0, CORE - 2 * EDGE)))
+            parts.append(joined(ch, *bands[1]))
+            tot[ch] = cat_rows([x for x, _ in parts])
+            margin = squeeze(cat_rows([x for _, x in parts]), n)
+            ptot[s] = margin if n == 0 else ptot[s] + margin
+
+    def incoming(x, turned=False):
+        even, thin = is_even(block), is_even((EDGE, CORE))
+        from_up, from_low = jnp.where(row < HALO - NEAR, x, 0.0), jnp.where(row > 0, x, 0.0)
+        rim_low, rim_up = jnp.where(sub < REACH, x[lo : lo + EDGE], 0.0), jnp.where(sub >= EDGE - REACH, x[hi : hi + EDGE], 0.0)
+        if turned:
+            return jnp.where(even, from_up, from_low), jnp.where(thin, rim_up, rim_low)
+        return jnp.where(even, from_low, from_up), jnp.where(thin, rim_low, rim_up)
+
+    def pass_on(ch):
+        s, n = divmod(ch, 2)
+        if ch not in DIRECT_B:
             upward[ch].got()
-            fill, rim = incoming(side_in[ch])
-            mate_out[ch, :CORE] += fill
+            more, rim = incoming(side_in[ch])
+            mate_out[ch, :CORE] += more
             mate_out[ch, CORE:] += rim
             onward[ch] = wire("mate", mate_out.at[ch], mate_in.at[ch])
             onward[ch].start()
+        if n == 0:
+            return
         upward[4 + s].got()
-        fill, rim = incoming(jnp.where(lane < FOLD, expand(pside_in[s]), 0.0))
-        pmate_out[s, :FOLD] = compact(pmate[s] + fill)
+        more, rim = incoming(jnp.where(lane < FOLD, expand(pside_in[s]), 0.0))
+        pmate_out[s, :FOLD] = compact(pmate[s] + more)
         pmate_out[s, FOLD:] = prim[s] + rim
         onward[4 + s] = wire("mate", pmate_out.at[s], pmate_in.at[s])
         onward[4 + s].start()
+
+    def total(ch):
+        onward[ch].got()
+        if ch not in DIRECT_B:
+            return cat_rows([tot[ch] + mate_in[ch, :CORE], edge[ch] + mate_in[ch, CORE:]])
+        upward[ch].got()
+        (a, ra), (b, rb) = incoming(near_in[ch]), incoming(side_in[ch], True)
+        return cat_rows([tot[ch] + a + b, edge[ch] + ra + rb])
 
     shape = (TVROWS, PROBE)
 
@@ -424,8 +478,7 @@
         pair = []
         for n in range(2):
             ch = 2 * s + n
-            onward[ch].got()
-            grad = cat_rows([tot[ch] + mate_in[ch, :CORE], edge[ch] + mate_in[ch, CORE:]])
+            grad = total(ch)
             grad = cat(grad, pltpu.roll(rest, CORE - REACH - 8 * n, 1), 1)
             wide = iota((EDGE, PROBE), 0) < EDGE // 2
             rim = jnp.where(wide, xs[ch, CORE : CORE + EDGE, :], xs[ch, PROBE - EDGE :, :])
@@ -451,7 +504,9 @@
     gr_, gi_ = inverse(tab, kr * fr + ki * fi, kr * fi - ki * fr)
     put(0, pr * gr_ + pi * gi_)
     put(1, pr * gi_ - pi * gr_)
-    fold(1)
+    inner = {s: cross(pl.ds(2 * s, 2), body_rows) for s in (1, 0)}
+    fold(2)
+    fold(3)
     for c in w_sides:
         c.got()
     row_at, col_at = iota(shape, 0), iota(shape, 1)
@@ -463,16 +518,24 @@
     margins = [pltpu.roll(m, CORE - REACH, 1) for m in margins]
     far = jnp.where(iota((TVROWS, CORE), 1) < HALF // 2, margins[0], margins[1])
     weight = cat(cat_rows([w[...], w_edge]), far, 1) * inside
+    fold(0)
+    pass_on(2)
+    pass_on(3)
+    fold(1)
+    pass_on(0)
     pass_on(1)
-    fold(0)
+    fill(1)
     smooth(1)
-    pass_on(0)
+    fill(0)
     smooth(0)
+    assert wire.count == COPIES
     for c in wire.all:
         c.sent()
 
 
-DIRECT_A = ()
+COPIES = 50
+DIRECT_A = (3,)
+DIRECT_B = (0, 2)
 
 
 def body(transmission, probe, fresnel_phase, amplitudes, positions, tv_weight):
@@ -484,10 +547,9 @@
 
     four = lambda n: [scratch(4, CORE, CORE)] * n
     small = lambda n: [scratch(EDGE, CORE)] * n
-    count = 48
     out = pl.pallas_call(
         whole_kernel,
-        out_shape=jax.ShapeDtypeStruct((4, CORE, CORE), F32),
+        out_shape=pltpu.VMEM((4, CORE, CORE), F32),
         in_specs=[anywhere] * 7,
         out_specs=vmem,
         scratch_shapes=[
@@ -496,12 +558,12 @@
             *four(8), *small(3), scratch(4, PROBE, PROBE),
             *[scratch(2 * EDGE, CORE)] * 3, *[scratch(FOLD + EDGE, CORE)] * 3,
             scratch(4, PROBE, PROBE), *[scratch(4, PROBE, CORE)] * 4,
-            scratch(4, CORE, CORE), scratch(4, EDGE, CORE), *four(2), *[scratch(4, TVROWS, CORE)] * 2,
+            scratch(4, CORE, CORE), scratch(4, EDGE, CORE), *four(4), *[scratch(4, TVROWS, CORE)] * 2,
             scratch(2, CORE, CORE), scratch(2, EDGE, CORE), scratch(2, CORE, CORE), scratch(2, EDGE, CORE),
             *[scratch(2, FOLD, CORE)] * 2,
             *[scratch(2, FOLD + EDGE, CORE)] * 2,
-            pltpu.SemaphoreType.DMA((count + 8,)),
-            pltpu.SemaphoreType.DMA((count + 8,)),
+            pltpu.SemaphoreType.DMA((len(OPPOSITE),)),
+            pltpu.SemaphoreType.DMA((COPIES,)),
             pltpu.SemaphoreType.DMA((7,)),
         ],
         compiler_params=pltpu.CompilerParams(collective_id=0, has_side_effects=True),

time: 41.5 us -> 34.2 us (0.82)
  Pallas kernels: 39.7 us -> 33 us
  local copies, waits for them, and re-layouts: 1.67 us -> 0.71 us
    pallas_call x1, Pallas kernels: 39.7 us -> 33 us  [body(): pl.pallas_call(whole_kernel, out_shape=pltpu.VMEM((4, CORE, CORE), F32),...]
    unnamed x1, local copies, waits for them, and re-layouts: 1.67 us -> 0.71 us
where the time goes in v2:
time: 34.2 us; the launch traced here: 33.7 us
  Pallas kernels  33 us (96%)
  local copies, waits for them, and re-layouts  0.71 us (2%)
    pallas_call x1, Pallas kernels, body(): pl.pallas_call(whole_kernel, out_shape=pltpu.VMEM((4, CORE, CORE), F32),...  33 us
    unnamed x1, local copies, waits for them, and re-layouts  0.71 us

profile of v2, /device:TPU:1, one launch (start us, length us, event | category | flops | bytes accessed | tf_op | source)
XLA Modules:
  0.0 33.7 jit_solution(1446355613427724135)
XLA Ops:
  0.0 33.0 %ptycho.1 = f32[4,128,128]{2,1,0:T(8,128)S(1)} custom-call(s32[2]{0:T(128)} %bitcast.7, f32[4,128,128]{2,1,0:T(8,128)} %bitcast.5, f32[128,128]{1,0:T(8,128)} %w_any.1, f32[2,256,256]{2,1,0:T(8,128)} %probe_any.1, f32[256,256]{1,0:T(8,128)} %phase_any.1, f32[256,256]{1,0:T(8,128)} %bitcast.6, bf16[10,256,256]{2,1,0:T(8,128)(2,1)} %constant.2.clone.tab_any), custom_call_target="tpu_custom_call" | custom-call | tf_op jit(solution)/shard_map/ptycho/pallas_call | solution.py:550
  33.0 0.7 %copy.9 = f32[2,2,128,128]{3,2,1,0:T(8,128)} copy(f32[2,2,128,128]{3,2,1,0:T(8,128)S(1)} %bitcast.4) | data formatting | bytes 524288

commit v3 on v2

--- a/solution.py
+++ b/solution.py
@@ -141,8 +141,9 @@
         self.place, self.send, self.recv = place, send, recv
         self.count, self.all = 0, []
 
-    def __call__(self, side, src, dst):
+    def __call__(self, side, src, dst, sends=True, gets=True):
         copy = Copy(self.place, side, src, dst, self.send.at[list(OPPOSITE).index(side)], self.recv.at[self.count])
+        copy.sends, copy.gets = copy.sends & sends, copy.gets & gets
         self.count += 1
         self.all.append(copy)
         return copy
@@ -195,10 +196,10 @@
 def whole_kernel(
     pos_any, tr_any, w_any, probe_any, phase_any, amp_any, tab_any, out,
     pos, tile, w, probe, phase_ref, amp, tab,
-    hl, hr, cl, cr, mt, nm, outl, outr, place_me, place_l, place_r, xs,
+    hl, hr, cl, cr, mt, nm, bridge, outl, outr, place_me, place_l, place_r, xs,
     w_rows, w_mate, w_other, w_pack, w_left, w_right,
     g, gl, gr, il, ir, tot, edge, side_out, side_in, near_out, near_in, mate_out, mate_in,
-    ptot, pedge, pmate, prim, pside_out, pside_in, pmate_out, pmate_in,
+    ptot, pedge, pside_out, pside_in, pnear_out, pnear_in,
     send, recv, local,
 ):
     place = Place()
@@ -215,13 +216,20 @@
     wire = Wire(place, send, recv)
     for side, refs in (
         ("left", (hl, cl, il, place_l, w_left)), ("right", (hr, cr, ir, place_r, w_right)),
-        ("other", (nm, w_other, *(side_in.at[ch] for ch in DIRECT_B))),
-        ("ahead", (pside_in, *(side_in.at[ch] for ch in range(4) if ch not in DIRECT_B))),
+        ("other", (nm, w_other, pside_in, *(side_in.at[ch] for ch in DIRECT_B), *(mate_in.at[ch] for ch in range(4) if ch not in DIRECT_B))),
+        ("ahead", tuple(side_in.at[ch] for ch in range(4) if ch not in DIRECT_B)),
     ):
         @pl.when(jnp.logical_not(has[side]))
         def _():
             for ref in refs:
                 ref[...] = jnp.zeros(ref.shape, F32)
+
+    @pl.when(has["other"])
+    def _():
+        for ch in range(4):
+            if ch not in DIRECT_B:
+                near_in[ch] = jnp.zeros((CORE, CORE), F32)
+
     loads[1].wait()
     p, q = pos[0], pos[1]
     place_me[...] = jnp.full((EDGE, CORE), p.astype(F32))
@@ -231,11 +239,19 @@
     low_strip = pl.ds(pl.multiple_of((CORE - STRIP) * odd, EDGE), STRIP)
     high_strip = pl.ds(pl.multiple_of((CORE - STRIP) * (1 - odd), EDGE), STRIP)
     direct = {ch: wire("other", tile.at[ch, low_strip], nm.at[ch, low_strip]) for ch in DIRECT_A}
-    to_mate = [wire("mate", tile.at[ch], mt.at[ch]) for ch in range(4)]
+    to_mate = [
+        wire("mate", *(ref.at[ch, high_strip if ch in (*direct, *VIA) else pl.ds(0, CORE)] for ref in (tile, mt))) for ch in range(4)
+    ]
     slices = [pl.ds(2 * s, 2) for s in range(2)]
     to_left = [wire("left", tile.at[part], hr.at[part]) for part in slices]
     to_right = [wire("right", tile.at[part], hl.at[part]) for part in slices]
-    relay = {ch: wire("ahead", mt.at[ch, high_strip], nm.at[ch, high_strip]) for ch in range(4) if ch not in direct}
+    via = {ch: wire("behind", tile.at[ch, low_strip], bridge.at[ch, low_strip]) for ch in VIA}
+    across_via = {
+        ch: wire("mate", bridge.at[ch, low_strip], nm.at[ch, low_strip], has["ahead"], has["other"]) for ch in VIA
+    }
+    relay = {
+        ch: wire("ahead", mt.at[ch, high_strip], nm.at[ch, high_strip]) for ch in range(4) if ch not in (*direct, *via)
+    }
     spots = [wire("left", place_me, place_r), wire("right", place_me, place_l)]
     corner_left = [wire("left", outl.at[ch], cr.at[ch]) for ch in range(4)]
     corner_right = [wire("right", outr.at[ch], cl.at[ch]) for ch in range(4)]
@@ -243,9 +259,11 @@
     w_sides = [wire("left", w_pack, w_right), wire("right", w_pack, w_left)]
     for c in spots:
         c.start()
-    for ch in range(4):
+    for ch in ORDER:
         if ch in direct:
             direct[ch].start()
+        if ch in via:
+            via[ch].start()
         to_mate[ch].start()
         if ch % 2 == 0:
             to_left[ch // 2].start()
@@ -273,6 +291,11 @@
             if ch in relay:
                 relay[ch].start()
 
+    def forward_via(channels):
+        for ch in channels:
+            via[ch].got()
+            across_via[ch].start()
+
     def forward_corners(channels):
         if 0 in channels:
             for c in spots:
@@ -280,7 +303,7 @@
         to_l = sign * (row - tall(place_l[...])) < 0
         to_r = sign * (row - tall(place_r[...])) < 0
         for ch in channels:
-            (direct[ch] if ch in direct else relay[ch]).got()
+            {**direct, **across_via, **relay}[ch].got()
             m, n = mt[ch], nm[ch]
             outl[ch] = jnp.where(to_l, m, n)
             corner_left[ch].start()
@@ -305,18 +328,19 @@
     phase = reorder(tab, phase_ref[...])
     kr, ki = jnp.cos(phase), jnp.sin(phase)
     forward_rows((0,))
-    forward_rows((1,))
+    forward_via(VIA)
+    forward_rows((2,))
     forward_corners((0,))
     loads[5].wait()
     turn_rows, turn_cols = p + (PROBE - HALO), q + (PROBE - HALO)
     pr, pi = (pltpu.roll(pltpu.roll(probe[n], turn_rows, 0), turn_cols, 1) for n in range(2))
+    forward_rows((1,))
     forward_corners((1,))
-    forward_rows((2,))
     loads[4].wait()
     measured = reorder(tab, amp[...])
+    forward_corners((2,))
     forward_rows((3,))
     forward_corners((3,))
-    forward_corners((2,))
     assemble(0)
     assemble(1)
     ar, ai = xs[0], xs[1]
@@ -336,7 +360,7 @@
     w_pack[FOLD:] = squeeze(w_edge, 0)
     for c in w_sides:
         c.start()
-    factor = 1.0 - measured / jnp.sqrt(fr * fr + fi * fi + AMP_EPS)
+    factor = 1.0 - measured * lax.rsqrt(fr * fr + fi * fi + AMP_EPS)
     gr_, gi_ = inverse(tab, fr * factor, fi * factor)
 
     across = {}
@@ -359,7 +383,7 @@
             c.start()
         return pair
 
-    upward, onward = {}, {}
+    upward, onward, beside = {}, {}, {}
 
     lo, hi = CORE - STRIP, STRIP - EDGE
 
@@ -398,17 +422,18 @@
         up = sum(jnp.where(m, 0.0, x) for m, x in parts)
         ends = [joined(ch, *band) for band in bands]
         rim, far, near, base, mate_rim = shares(ends[0][0], ends[1][0], down, up)
-        edge[ch], side_out[ch] = rim, far
+        edge[ch], side_out[ch], near_out[ch] = rim, far, near
+        strip = side_out.at[ch, high_strip], side_in.at[ch, high_strip]
+        near_strip = near_out.at[ch, low_strip], near_in.at[ch, low_strip]
         if ch in DIRECT_B:
-            near_out[ch] = near
-            upward[ch] = wire("other", side_out.at[ch, high_strip], side_in.at[ch, high_strip])
-            onward[ch] = wire("mate", near_out.at[ch, low_strip], near_in.at[ch, low_strip])
-            upward[ch].start()
-            onward[ch].start()
+            upward[ch] = wire("other", *strip)
+            beside[ch] = wire("mate", *near_strip)
         else:
-            upward[ch] = wire("behind", side_out.at[ch, high_strip], side_in.at[ch, high_strip])
-            upward[ch].start()
+            upward[ch] = wire("behind", *strip)
+            beside[ch] = wire("mate", *near_strip, jnp.logical_not(has["ahead"]), jnp.logical_not(has["other"]))
             mate_out[ch, :CORE], mate_out[ch, CORE:] = base, mate_rim
+        upward[ch].start()
+        beside[ch].start()
         o = jnp.where(low, fr, fl)
         pieces = [
             ends[0][1], ends[1][1],
@@ -419,10 +444,12 @@
         if n == 0:
             packs[s] = pieces
             return
-        pedge[s], far, _, pmate[s], prim[s] = shares(*[a + b for a, b in zip(packs[s], pieces)])
-        pside_out[s] = compact(far)
-        upward[4 + s] = wire("behind", pside_out.at[s], pside_in.at[s])
+        pedge[s], far, near, _, _ = shares(*[a + b for a, b in zip(packs[s], pieces)])
+        pside_out[s], pnear_out[s] = compact(far), compact(near)
+        upward[4 + s] = wire("other", pside_out.at[s], pside_in.at[s])
+        beside[4 + s] = wire("mate", pnear_out.at[s], pnear_in.at[s])
         upward[4 + s].start()
+        beside[4 + s].start()
 
     def fill(s):
         for c in inner[s]:
@@ -445,36 +472,31 @@
         return jnp.where(even, from_low, from_up), jnp.where(thin, rim_low, rim_up)
 
     def pass_on(ch):
-        s, n = divmod(ch, 2)
-        if ch not in DIRECT_B:
+        upward[ch].got()
+        more, rim = incoming(side_in[ch])
+        mate_out[ch, :CORE] += more
+        mate_out[ch, CORE:] += rim
+        onward[ch] = wire("mate", mate_out.at[ch], mate_in.at[ch], has["ahead"], has["other"])
+        onward[ch].start()
+
+    def total(ch):
+        beside[ch].got()
+        a, ra = incoming(near_in[ch])
+        if ch in DIRECT_B:
             upward[ch].got()
-            more, rim = incoming(side_in[ch])
-            mate_out[ch, :CORE] += more
-            mate_out[ch, CORE:] += rim
-            onward[ch] = wire("mate", mate_out.at[ch], mate_in.at[ch])
-            onward[ch].start()
-        if n == 0:
-            return
+            b, rb = incoming(side_in[ch], True)
+        else:
+            onward[ch].got()
+            b, rb = mate_in[ch, :CORE], mate_in[ch, CORE:]
+        return cat_rows([tot[ch] + a + b, edge[ch] + ra + rb])
+
+    shape = (TVROWS, PROBE)
+
+    def smooth(s):
         upward[4 + s].got()
-        more, rim = incoming(jnp.where(lane < FOLD, expand(pside_in[s]), 0.0))
-        pmate_out[s, :FOLD] = compact(pmate[s] + more)
-        pmate_out[s, FOLD:] = prim[s] + rim
-        onward[4 + s] = wire("mate", pmate_out.at[s], pmate_in.at[s])
-        onward[4 + s].start()
-
-    def total(ch):
-        onward[ch].got()
-        if ch not in DIRECT_B:
-            return cat_rows([tot[ch] + mate_in[ch, :CORE], edge[ch] + mate_in[ch, CORE:]])
-        upward[ch].got()
-        (a, ra), (b, rb) = incoming(near_in[ch]), incoming(side_in[ch], True)
-        return cat_rows([tot[ch] + a + b, edge[ch] + ra + rb])
-
-    shape = (TVROWS, PROBE)
-
-    def smooth(s):
-        onward[4 + s].got()
-        rest = cat_rows([ptot[s] + expand(pmate_in[s, :FOLD]), pedge[s] + pmate_in[s, FOLD:]])
+        beside[4 + s].got()
+        (a, ra), (b, rb) = incoming(expand(pnear_in[s])), incoming(expand(pside_in[s]), True)
+        rest = cat_rows([ptot[s] + a + b, pedge[s] + ra + rb])
         pair = []
         for n in range(2):
             ch = 2 * s + n
@@ -488,7 +510,7 @@
             down = [pltpu.roll(f, TVROWS - 1, 0) - f for f in pair]
             along_row = [pltpu.roll(f, PROBE - 1, 1) - f for f in pair]
             square = down[0] * down[0] + along_row[0] * along_row[0] + (down[1] * down[1] + along_row[1] * along_row[1])
-            gain = weight / jnp.sqrt(square + TV_EPS)
+            gain = weight * lax.rsqrt(square + TV_EPS)
             fresh = []
             for f, d, r in zip(pair, down, along_row):
                 d, r = gain * d, gain * r
@@ -519,11 +541,9 @@
     far = jnp.where(iota((TVROWS, CORE), 1) < HALF // 2, margins[0], margins[1])
     weight = cat(cat_rows([w[...], w_edge]), far, 1) * inside
     fold(0)
-    pass_on(2)
+    fold(1)
     pass_on(3)
-    fold(1)
     pass_on(0)
-    pass_on(1)
     fill(1)
     smooth(1)
     fill(0)
@@ -533,9 +553,11 @@
         c.sent()
 
 
-COPIES = 50
+COPIES = 53
+ORDER = (0, 2, 1, 3)
 DIRECT_A = (3,)
-DIRECT_B = (0, 2)
+VIA = (1,)
+DIRECT_B = (1, 2)
 
 
 def body(transmission, probe, fresnel_phase, amplitudes, positions, tv_weight):
@@ -555,13 +577,11 @@
         scratch_shapes=[
             pltpu.SMEM((2,), jnp.int32), scratch(4, CORE, CORE), scratch(CORE, CORE), scratch(2, PROBE, PROBE),
             scratch(PROBE, PROBE), scratch(PROBE, PROBE), pltpu.VMEM(tab.shape, BF16),
-            *four(8), *small(3), scratch(4, PROBE, PROBE),
+            *four(9), *small(3), scratch(4, PROBE, PROBE),
             *[scratch(2 * EDGE, CORE)] * 3, *[scratch(FOLD + EDGE, CORE)] * 3,
             scratch(4, PROBE, PROBE), *[scratch(4, PROBE, CORE)] * 4,
             scratch(4, CORE, CORE), scratch(4, EDGE, CORE), *four(4), *[scratch(4, TVROWS, CORE)] * 2,
-            scratch(2, CORE, CORE), scratch(2, EDGE, CORE), scratch(2, CORE, CORE), scratch(2, EDGE, CORE),
-            *[scratch(2, FOLD, CORE)] * 2,
-            *[scratch(2, FOLD + EDGE, CORE)] * 2,
+            scratch(2, CORE, CORE), scratch(2, EDGE, CORE), *[scratch(2, FOLD, CORE)] * 4,
             pltpu.SemaphoreType.DMA((len(OPPOSITE),)),
             pltpu.SemaphoreType.DMA((COPIES,)),
             pltpu.SemaphoreType.DMA((7,)),

time: 34.2 us -> 32.8 us (0.959)
  Pallas kernels: 33 us -> 31.6 us
    pallas_call x1, Pallas kernels: 33 us -> 31.6 us  [body(): pl.pallas_call(whole_kernel, out_shape=pltpu.VMEM((4, CORE, CORE), F32),...]
where the time goes in v3:
time: 32.8 us; the launch traced here: 32.3 us
  Pallas kernels  31.6 us (96%)
  local copies, waits for them, and re-layouts  0.71 us (2%)
    pallas_call x1, Pallas kernels, body(): pl.pallas_call(whole_kernel, out_shape=pltpu.VMEM((4, CORE, CORE), F32),...  31.6 us
    unnamed x1, local copies, waits for them, and re-layouts  0.71 us

profile of v3, /device:TPU:1, one launch (start us, length us, event | category | flops | bytes accessed | tf_op | source)
XLA Modules:
  0.0 32.3 jit_solution(1203957476440304245)
XLA Ops:
  0.0 31.6 %ptycho.1 = f32[4,128,128]{2,1,0:T(8,128)S(1)} custom-call(s32[2]{0:T(128)} %bitcast.7, f32[4,128,128]{2,1,0:T(8,128)} %bitcast.5, f32[128,128]{1,0:T(8,128)} %w_any.1, f32[2,256,256]{2,1,0:T(8,128)} %probe_any.1, f32[256,256]{1,0:T(8,128)} %phase_any.1, f32[256,256]{1,0:T(8,128)} %bitcast.6, bf16[10,256,256]{2,1,0:T(8,128)(2,1)} %constant.2.clone.tab_any), custom_call_target="tpu_custom_call" | custom-call | tf_op jit(solution)/shard_map/ptycho/pallas_call | solution.py:572
  31.6 0.7 %copy.9 = f32[2,2,128,128]{3,2,1,0:T(8,128)} copy(f32[2,2,128,128]{3,2,1,0:T(8,128)S(1)} %bitcast.4) | data formatting | bytes 524288

commit v4 on v3

--- a/solution.py
+++ b/solution.py
@@ -259,11 +259,11 @@
     w_sides = [wire("left", w_pack, w_right), wire("right", w_pack, w_left)]
     for c in spots:
         c.start()
+    for ch in VIA:
+        via[ch].start()
     for ch in ORDER:
         if ch in direct:
             direct[ch].start()
-        if ch in via:
-            via[ch].start()
         to_mate[ch].start()
         if ch % 2 == 0:
             to_left[ch // 2].start()
@@ -327,20 +327,17 @@
     loads[3].wait()
     phase = reorder(tab, phase_ref[...])
     kr, ki = jnp.cos(phase), jnp.sin(phase)
-    forward_rows((0,))
-    forward_via(VIA)
-    forward_rows((2,))
-    forward_corners((0,))
     loads[5].wait()
     turn_rows, turn_cols = p + (PROBE - HALO), q + (PROBE - HALO)
     pr, pi = (pltpu.roll(pltpu.roll(probe[n], turn_rows, 0), turn_cols, 1) for n in range(2))
-    forward_rows((1,))
-    forward_corners((1,))
+    forward_via(VIA)
+    forward_rows((0,))
+    forward_corners((0,))
     loads[4].wait()
     measured = reorder(tab, amp[...])
-    forward_corners((2,))
-    forward_rows((3,))
-    forward_corners((3,))
+    for ch in (1, 2, 3):
+        forward_rows((ch,))
+        forward_corners((ch,))
     assemble(0)
     assemble(1)
     ar, ai = xs[0], xs[1]
@@ -553,10 +550,10 @@
         c.sent()
 
 
-COPIES = 53
-ORDER = (0, 2, 1, 3)
-DIRECT_A = (3,)
-VIA = (1,)
+COPIES = 54
+ORDER = (0, 1, 2, 3)
+DIRECT_A = (0, 1)
+VIA = (2, 3)
 DIRECT_B = (1, 2)
 
 

time: 32.8 us -> 31.3 us (0.954)
  the two profiles are of different devices: /device:TPU:1 before, /device:TPU:10 now
where the time goes in v4:
time: 31.3 us; the launch traced here: 31.1 us
  Pallas kernels  30.4 us (97%)
  local copies, waits for them, and re-layouts  0.71 us (2%)
    pallas_call x1, Pallas kernels, body(): pl.pallas_call(whole_kernel, out_shape=pltpu.VMEM((4, CORE, CORE), F32),...  30.4 us
    unnamed x1, local copies, waits for them, and re-layouts  0.71 us

profile of v4, /device:TPU:10, one launch (start us, length us, event | category | flops | bytes accessed | tf_op | source)
XLA Modules:
  0.0 31.1 jit_solution(3981438846000955244)
XLA Ops:
  0.0 30.4 %ptycho.1 = f32[4,128,128]{2,1,0:T(8,128)S(1)} custom-call(s32[2]{0:T(128)} %bitcast.7, f32[4,128,128]{2,1,0:T(8,128)} %bitcast.5, f32[128,128]{1,0:T(8,128)} %w_any.1, f32[2,256,256]{2,1,0:T(8,128)} %probe_any.1, f32[256,256]{1,0:T(8,128)} %phase_any.1, f32[256,256]{1,0:T(8,128)} %bitcast.6, bf16[10,256,256]{2,1,0:T(8,128)(2,1)} %constant.2.clone.tab_any), custom_call_target="tpu_custom_call" | custom-call | tf_op jit(solution)/shard_map/ptycho/pallas_call | solution.py:569
  30.4 0.7 %copy.9 = f32[2,2,128,128]{3,2,1,0:T(8,128)} copy(f32[2,2,128,128]{3,2,1,0:T(8,128)S(1)} %bitcast.4) | data formatting | bytes 524288

commit v5 on v4

--- a/solution.py
+++ b/solution.py
@@ -199,7 +199,7 @@
     hl, hr, cl, cr, mt, nm, bridge, outl, outr, place_me, place_l, place_r, xs,
     w_rows, w_mate, w_other, w_pack, w_left, w_right,
     g, gl, gr, il, ir, tot, edge, side_out, side_in, near_out, near_in, mate_out, mate_in,
-    ptot, pedge, pside_out, pside_in, pnear_out, pnear_in,
+    fields, ptot, pedge, pbridge, pside_out, pside_in, pnear_out, pnear_in,
     send, recv, local,
 ):
     place = Place()
@@ -238,6 +238,9 @@
 
     low_strip = pl.ds(pl.multiple_of((CORE - STRIP) * odd, EDGE), STRIP)
     high_strip = pl.ds(pl.multiple_of((CORE - STRIP) * (1 - odd), EDGE), STRIP)
+    half_strips = [
+        pl.ds(pl.multiple_of((CORE - STRIP) * (1 - odd) + at, EDGE), size) for at, size in ((0, CUT), (CUT, STRIP - CUT))
+    ]
     direct = {ch: wire("other", tile.at[ch, low_strip], nm.at[ch, low_strip]) for ch in DIRECT_A}
     to_mate = [
         wire("mate", *(ref.at[ch, high_strip if ch in (*direct, *VIA) else pl.ds(0, CORE)] for ref in (tile, mt))) for ch in range(4)
@@ -380,7 +383,7 @@
             c.start()
         return pair
 
-    upward, onward, beside = {}, {}, {}
+    upward, onward, beside, bridged = {}, {}, {}, {}
 
     lo, hi = CORE - STRIP, STRIP - EDGE
 
@@ -421,15 +424,17 @@
         rim, far, near, base, mate_rim = shares(ends[0][0], ends[1][0], down, up)
         edge[ch], side_out[ch], near_out[ch] = rim, far, near
         strip = side_out.at[ch, high_strip], side_in.at[ch, high_strip]
+        halves = [(side_out.at[ch, rows], side_in.at[ch, rows]) for rows in half_strips]
         near_strip = near_out.at[ch, low_strip], near_in.at[ch, low_strip]
         if ch in DIRECT_B:
             upward[ch] = wire("other", *strip)
             beside[ch] = wire("mate", *near_strip)
         else:
-            upward[ch] = wire("behind", *strip)
+            upward[ch] = [wire("behind", *half) for half in halves]
             beside[ch] = wire("mate", *near_strip, jnp.logical_not(has["ahead"]), jnp.logical_not(has["other"]))
             mate_out[ch, :CORE], mate_out[ch, CORE:] = base, mate_rim
-        upward[ch].start()
+        for c in [upward[ch]] if ch in DIRECT_B else upward[ch]:
+            c.start()
         beside[ch].start()
         o = jnp.where(low, fr, fl)
         pieces = [
@@ -443,10 +448,15 @@
             return
         pedge[s], far, near, _, _ = shares(*[a + b for a, b in zip(packs[s], pieces)])
         pside_out[s], pnear_out[s] = compact(far), compact(near)
-        upward[4 + s] = wire("other", pside_out.at[s], pside_in.at[s])
+        bridged[s] = wire("behind", pside_out.at[s], pbridge.at[s])
+        upward[4 + s] = wire("mate", pbridge.at[s], pside_in.at[s], has["ahead"], has["other"])
         beside[4 + s] = wire("mate", pnear_out.at[s], pnear_in.at[s])
+        bridged[s].start()
+        beside[4 + s].start()
+
+    def pass_pack(s):
+        bridged[s].got()
         upward[4 + s].start()
-        beside[4 + s].start()
 
     def fill(s):
         for c in inner[s]:
@@ -469,12 +479,18 @@
         return jnp.where(even, from_low, from_up), jnp.where(thin, rim_low, rim_up)
 
     def pass_on(ch):
-        upward[ch].got()
-        more, rim = incoming(side_in[ch])
-        mate_out[ch, :CORE] += more
-        mate_out[ch, CORE:] += rim
-        onward[ch] = wire("mate", mate_out.at[ch], mate_in.at[ch], has["ahead"], has["other"])
-        onward[ch].start()
+        onward[ch] = []
+        for n, rows in enumerate((pl.ds(0, CUT), pl.ds(CUT, TVROWS - CUT))):
+            upward[ch][n].got()
+            if n == 0:
+                x = side_in[ch, :CUT]
+                mate_out[ch, :CUT] += jnp.where(is_even(x.shape), jnp.where(row[:CUT] > 0, x, 0.0), x)
+            else:
+                more, rim = incoming(side_in[ch])
+                mate_out[ch, CUT:CORE] += more[CUT:]
+                mate_out[ch, CORE:] += rim
+            onward[ch].append(wire("mate", mate_out.at[ch, rows], mate_in.at[ch, rows], has["ahead"], has["other"]))
+            onward[ch][n].start()
 
     def total(ch):
         beside[ch].got()
@@ -483,26 +499,32 @@
             upward[ch].got()
             b, rb = incoming(side_in[ch], True)
         else:
-            onward[ch].got()
+            for c in onward[ch]:
+                c.got()
             b, rb = mate_in[ch, :CORE], mate_in[ch, CORE:]
-        return cat_rows([tot[ch] + a + b, edge[ch] + ra + rb])
+        return cat_rows([a + b, ra + rb])
 
     shape = (TVROWS, PROBE)
+
+    def prepare(s):
+        rest = cat_rows([ptot[s], pedge[s]])
+        for n in range(2):
+            ch = 2 * s + n
+            grad = cat(cat_rows([tot[ch], edge[ch]]), pltpu.roll(rest, CORE - REACH - 8 * n, 1), 1)
+            wide = iota((EDGE, PROBE), 0) < EDGE // 2
+            rim = jnp.where(wide, xs[ch, CORE : CORE + EDGE, :], xs[ch, PROBE - EDGE :, :])
+            fields[ch] = (cat_rows([xs[ch, :CORE, :], rim]) - LEARN_RATE * grad) * inside
 
     def smooth(s):
         upward[4 + s].got()
         beside[4 + s].got()
         (a, ra), (b, rb) = incoming(expand(pnear_in[s])), incoming(expand(pside_in[s]), True)
-        rest = cat_rows([ptot[s] + a + b, pedge[s] + ra + rb])
+        rest = cat_rows([a + b, ra + rb])
         pair = []
         for n in range(2):
             ch = 2 * s + n
-            grad = total(ch)
-            grad = cat(grad, pltpu.roll(rest, CORE - REACH - 8 * n, 1), 1)
-            wide = iota((EDGE, PROBE), 0) < EDGE // 2
-            rim = jnp.where(wide, xs[ch, CORE : CORE + EDGE, :], xs[ch, PROBE - EDGE :, :])
-            field = cat_rows([xs[ch, :CORE, :], rim])
-            pair.append((field - LEARN_RATE * grad) * inside)
+            grad = cat(total(ch), pltpu.roll(rest, CORE - REACH - 8 * n, 1), 1)
+            pair.append(fields[ch] - LEARN_RATE * inside * grad)
         for _ in range(TV_STEPS):
             down = [pltpu.roll(f, TVROWS - 1, 0) - f for f in pair]
             along_row = [pltpu.roll(f, PROBE - 1, 1) - f for f in pair]
@@ -539,22 +561,27 @@
     weight = cat(cat_rows([w[...], w_edge]), far, 1) * inside
     fold(0)
     fold(1)
-    pass_on(3)
+    pass_on(2)
+    pass_pack(1)
     pass_on(0)
+    pass_pack(0)
     fill(1)
+    prepare(1)
+    fill(0)
+    prepare(0)
     smooth(1)
-    fill(0)
     smooth(0)
     assert wire.count == COPIES
     for c in wire.all:
         c.sent()
 
 
-COPIES = 54
+COPIES = 60
+CUT = 56
 ORDER = (0, 1, 2, 3)
 DIRECT_A = (0, 1)
 VIA = (2, 3)
-DIRECT_B = (1, 2)
+DIRECT_B = (1, 3)
 
 
 def body(transmission, probe, fresnel_phase, amplitudes, positions, tv_weight):
@@ -578,7 +605,7 @@
             *[scratch(2 * EDGE, CORE)] * 3, *[scratch(FOLD + EDGE, CORE)] * 3,
             scratch(4, PROBE, PROBE), *[scratch(4, PROBE, CORE)] * 4,
             scratch(4, CORE, CORE), scratch(4, EDGE, CORE), *four(4), *[scratch(4, TVROWS, CORE)] * 2,
-            scratch(2, CORE, CORE), scratch(2, EDGE, CORE), *[scratch(2, FOLD, CORE)] * 4,
+            scratch(4, TVROWS, PROBE), scratch(2, CORE, CORE), scratch(2, EDGE, CORE), *[scratch(2, FOLD, CORE)] * 5,
             pltpu.SemaphoreType.DMA((len(OPPOSITE),)),
             pltpu.SemaphoreType.DMA((COPIES,)),
             pltpu.SemaphoreType.DMA((7,)),

time: 31.3 us -> 30.5 us (0.974)
  the two profiles are of different devices: /device:TPU:10 before, /device:TPU:1 now
where the time goes in v5:
time: 30.5 us; the launch traced here: 30 us
  Pallas kernels  29.3 us (96%)
  local copies, waits for them, and re-layouts  0.71 us (2%)
    pallas_call x1, Pallas kernels, body(): pl.pallas_call(whole_kernel, out_shape=pltpu.VMEM((4, CORE, CORE), F32),...  29.3 us
    unnamed x1, local copies, waits for them, and re-layouts  0.71 us

profile of v5, /device:TPU:1, one launch (start us, length us, event | category | flops | bytes accessed | tf_op | source)
XLA Modules:
  0.0 30.0 jit_solution(10589242035806075068)
XLA Ops:
  0.0 29.3 %ptycho.1 = f32[4,128,128]{2,1,0:T(8,128)S(1)} custom-call(s32[2]{0:T(128)} %bitcast.7, f32[4,128,128]{2,1,0:T(8,128)} %bitcast.5, f32[128,128]{1,0:T(8,128)} %w_any.1, f32[2,256,256]{2,1,0:T(8,128)} %probe_any.1, f32[256,256]{1,0:T(8,128)} %phase_any.1, f32[256,256]{1,0:T(8,128)} %bitcast.6, bf16[10,256,256]{2,1,0:T(8,128)(2,1)} %constant.2.clone.tab_any), custom_call_target="tpu_custom_call" | custom-call | tf_op jit(solution)/shard_map/ptycho/pallas_call | solution.py:596
  29.3 0.7 %copy.9 = f32[2,2,128,128]{3,2,1,0:T(8,128)} copy(f32[2,2,128,128]{3,2,1,0:T(8,128)S(1)} %bitcast.4) | data formatting | bytes 524288

commit v6 on v5

--- a/solution.py
+++ b/solution.py
@@ -504,40 +504,68 @@
             b, rb = mate_in[ch, :CORE], mate_in[ch, CORE:]
         return cat_rows([a + b, ra + rb])
 
-    shape = (TVROWS, PROBE)
+
+    slab = (TVROWS, CORE)
+    turn = CORE // 2
+
+    def both(first, second):
+        at = iota(slab, 1)
+        return jnp.where((at >= turn // 2) & (at < turn + turn // 2), second, first)
+
+    def unpack(rest):
+        return both(pltpu.roll(rest, CORE - REACH, 1), pltpu.roll(rest, turn - REACH - 8, 1))
+
+    def kept(x):
+        return cat_rows([x[:CORE], x[CORE:] * in_rim])
 
     def prepare(s):
-        rest = cat_rows([ptot[s], pedge[s]])
+        sides = []
         for n in range(2):
             ch = 2 * s + n
-            grad = cat(cat_rows([tot[ch], edge[ch]]), pltpu.roll(rest, CORE - REACH - 8 * n, 1), 1)
             wide = iota((EDGE, PROBE), 0) < EDGE // 2
             rim = jnp.where(wide, xs[ch, CORE : CORE + EDGE, :], xs[ch, PROBE - EDGE :, :])
-            fields[ch] = (cat_rows([xs[ch, :CORE, :], rim]) - LEARN_RATE * grad) * inside
+            grad = cat_rows([tot[ch], edge[ch]])
+            fields[s, n] = kept(cat_rows([xs[ch, :CORE, :CORE], rim[:, :CORE]]) - LEARN_RATE * grad)
+            sides.append(cat_rows([xs[ch, :CORE, CORE:], rim[:, CORE:]]))
+        side = both(sides[0], pltpu.roll(sides[1], turn, 1))
+        fields[s, 2] = (side - LEARN_RATE * unpack(cat_rows([ptot[s], pedge[s]]))) * side_inside
 
     def smooth(s):
         upward[4 + s].got()
         beside[4 + s].got()
         (a, ra), (b, rb) = incoming(expand(pnear_in[s])), incoming(expand(pside_in[s]), True)
-        rest = cat_rows([a + b, ra + rb])
-        pair = []
+        side = fields[s, 2] - LEARN_RATE * side_inside * unpack(cat_rows([a + b, ra + rb]))
+        own = [fields[s, n] - LEARN_RATE * kept(total(2 * s + n)) for n in range(2)]
+        at = iota(slab, 1)
+        first, last = at == 0, at == CORE - 1
+        for _ in range(TV_STEPS):
+            three = (*own, side)
+            after = [pltpu.roll(f, CORE - 1, 1) for f in three]
+            right = [
+                jnp.where(last, after[2], after[0]),
+                jnp.where(last, pltpu.roll(side, turn - 1, 1), after[1]),
+                jnp.where(last, after[0], jnp.where(at == turn - 1, pltpu.roll(own[1], turn - 1, 1), after[2])),
+            ]
+            right = [x - f for x, f in zip(right, three)]
+            down = [pltpu.roll(f, TVROWS - 1, 0) - f for f in three]
+            squares = [d * d + r * r for d, r in zip(down, right)]
+            gain = weight * lax.rsqrt(squares[0] + squares[1] + TV_EPS)
+            side_gain = side_weight * lax.rsqrt(squares[2] + pltpu.roll(squares[2], turn, 1) + TV_EPS)
+            gains = (gain, gain, side_gain)
+            down = [k * d for k, d in zip(gains, down)]
+            right = [k * r for k, r in zip(gains, right)]
+            before = [pltpu.roll(r, 1, 1) for r in right]
+            left = [
+                jnp.where(first, before[2], before[0]),
+                jnp.where(first, pltpu.roll(right[2], turn + 1, 1), before[1]),
+                jnp.where(first, before[0], jnp.where(at == turn, pltpu.roll(right[1], turn + 1, 1), before[2])),
+            ]
+            fresh = [
+                f + (d - pltpu.roll(d, 1, 0) + (r - x)) for f, d, r, x in zip(three, down, right, left)
+            ]
+            own, side = [kept(f) for f in fresh[:2]], fresh[2] * side_inside
         for n in range(2):
-            ch = 2 * s + n
-            grad = cat(total(ch), pltpu.roll(rest, CORE - REACH - 8 * n, 1), 1)
-            pair.append(fields[ch] - LEARN_RATE * inside * grad)
-        for _ in range(TV_STEPS):
-            down = [pltpu.roll(f, TVROWS - 1, 0) - f for f in pair]
-            along_row = [pltpu.roll(f, PROBE - 1, 1) - f for f in pair]
-            square = down[0] * down[0] + along_row[0] * along_row[0] + (down[1] * down[1] + along_row[1] * along_row[1])
-            gain = weight * lax.rsqrt(square + TV_EPS)
-            fresh = []
-            for f, d, r in zip(pair, down, along_row):
-                d, r = gain * d, gain * r
-                update = d - pltpu.roll(d, 1, 0) + (r - pltpu.roll(r, 1, 1))
-                fresh.append((f + TV_TAU * update) * inside)
-            pair = fresh
-        for n in range(2):
-            out[2 * s + n] = pair[n][:CORE, :CORE]
+            out[2 * s + n] = own[n][:CORE]
 
     put(2, wr * gr_ + wi * gi_)
     put(3, wr * gi_ - wi * gr_)
@@ -550,15 +578,18 @@
     fold(3)
     for c in w_sides:
         c.got()
-    row_at, col_at = iota(shape, 0), iota(shape, 1)
+    row_at, col_at = iota(slab, 0), iota(slab, 1)
     row_at = place.r * CORE + jnp.where(row_at < CORE + EDGE // 2, row_at, row_at - TVROWS)
-    col_at = place.c * CORE + jnp.where(col_at < CORE + HALF // 2, col_at, col_at - PROBE)
-    inside = (row_at >= 0) & (row_at < place.nr * CORE) & (col_at >= 0) & (col_at < place.nc * CORE)
-    inside = inside.astype(F32)
+    col_at = both(col_at, col_at - turn + jnp.where(col_at < turn, CORE, 0))
+    col_at = place.c * CORE + jnp.where(col_at < turn, col_at + CORE, col_at - CORE)
+    in_rows = (row_at >= 0) & (row_at < place.nr * CORE)
+    side_inside = (in_rows & (col_at >= 0) & (col_at < place.nc * CORE)).astype(F32)
+    in_rim = in_rows.astype(F32)[CORE:]
     margins = [cat_rows([expand(ref[:FOLD]), ref[FOLD:]]) for ref in (w_right, w_left)]
     margins = [pltpu.roll(m, CORE - REACH, 1) for m in margins]
-    far = jnp.where(iota((TVROWS, CORE), 1) < HALF // 2, margins[0], margins[1])
-    weight = cat(cat_rows([w[...], w_edge]), far, 1) * inside
+    far = jnp.where(iota(slab, 1) < turn, margins[0], margins[1])
+    weight = TV_TAU * kept(cat_rows([w[...], w_edge]))
+    side_weight = TV_TAU * side_inside * both(far, pltpu.roll(far, turn, 1))
     fold(0)
     fold(1)
     pass_on(2)
@@ -605,7 +636,7 @@
             *[scratch(2 * EDGE, CORE)] * 3, *[scratch(FOLD + EDGE, CORE)] * 3,
             scratch(4, PROBE, PROBE), *[scratch(4, PROBE, CORE)] * 4,
             scratch(4, CORE, CORE), scratch(4, EDGE, CORE), *four(4), *[scratch(4, TVROWS, CORE)] * 2,
-            scratch(4, TVROWS, PROBE), scratch(2, CORE, CORE), scratch(2, EDGE, CORE), *[scratch(2, FOLD, CORE)] * 5,
+            scratch(2, 3, TVROWS, CORE), scratch(2, CORE, CORE), scratch(2, EDGE, CORE), *[scratch(2, FOLD, CORE)] * 5,
             pltpu.SemaphoreType.DMA((len(OPPOSITE),)),
             pltpu.SemaphoreType.DMA((COPIES,)),
             pltpu.SemaphoreType.DMA((7,)),

time: 30.5 us -> 30.6 us (level)
  no operation moved by 1% of the time
where the time goes in v6:
time: 30.6 us; the launch traced here: 30.1 us
  Pallas kernels  29.4 us (96%)
  local copies, waits for them, and re-layouts  0.71 us (2%)
    pallas_call x1, Pallas kernels, body(): pl.pallas_call(whole_kernel, out_shape=pltpu.VMEM((4, CORE, CORE), F32),...  29.4 us
    unnamed x1, local copies, waits for them, and re-layouts  0.71 us

profile of v6, /device:TPU:1, one launch (start us, length us, event | category | flops | bytes accessed | tf_op | source)
XLA Modules:
  0.0 30.1 jit_solution(9088050641510422615)
XLA Ops:
  0.0 29.4 %ptycho.1 = f32[4,128,128]{2,1,0:T(8,128)S(1)} custom-call(s32[2]{0:T(128)} %bitcast.7, f32[4,128,128]{2,1,0:T(8,128)} %bitcast.5, f32[128,128]{1,0:T(8,128)} %w_any.1, f32[2,256,256]{2,1,0:T(8,128)} %probe_any.1, f32[256,256]{1,0:T(8,128)} %phase_any.1, f32[256,256]{1,0:T(8,128)} %bitcast.6, bf16[10,256,256]{2,1,0:T(8,128)(2,1)} %constant.2.clone.tab_any), custom_call_target="tpu_custom_call" | custom-call | tf_op jit(solution)/shard_map/ptycho/pallas_call | solution.py:627
  29.4 0.7 %copy.9 = f32[2,2,128,128]{3,2,1,0:T(8,128)} copy(f32[2,2,128,128]{3,2,1,0:T(8,128)S(1)} %bitcast.4) | data formatting | bytes 524288

commit v7 on v5

--- a/solution.py
+++ b/solution.py
@@ -525,19 +525,56 @@
             ch = 2 * s + n
             grad = cat(total(ch), pltpu.roll(rest, CORE - REACH - 8 * n, 1), 1)
             pair.append(fields[ch] - LEARN_RATE * inside * grad)
-        for _ in range(TV_STEPS):
-            down = [pltpu.roll(f, TVROWS - 1, 0) - f for f in pair]
-            along_row = [pltpu.roll(f, PROBE - 1, 1) - f for f in pair]
-            square = down[0] * down[0] + along_row[0] * along_row[0] + (down[1] * down[1] + along_row[1] * along_row[1])
-            gain = weight * lax.rsqrt(square + TV_EPS)
-            fresh = []
-            for f, d, r in zip(pair, down, along_row):
-                d, r = gain * d, gain * r
-                update = d - pltpu.roll(d, 1, 0) + (r - pltpu.roll(r, 1, 1))
-                fresh.append((f + TV_TAU * update) * inside)
-            pair = fresh
-        for n in range(2):
-            out[2 * s + n] = pair[n][:CORE, :CORE]
+        march(s, pair)
+
+    def march(s, pair):
+        count = CORE // EDGE + 2
+        at = iota((EDGE, PROBE), 0)
+
+        def tiles(x):
+            rows = [x[EDGE * k : EDGE * k + EDGE] for k in range(TVROWS // EDGE)]
+            return rows[-1:] + rows
+
+        kept, weights = tiles(inside), tiles(TV_TAU * weight)
+        done = {(0, n, k): t for n in range(2) for k, t in enumerate(tiles(pair[0]) if n == 0 else tiles(pair[1]))}
+        memo = {}
+
+        def once(key, make):
+            if key not in memo:
+                memo[key] = make()
+            return memo[key]
+
+        def field(step, n, k):
+            if (step, n, k) not in done:
+                f = field(step - 1, n, k)
+                d, r = flux(step - 1, k)[n]
+                before = fallen(step - 1, n, k - 1) if k else fallen(step - 1, n, k)
+                d = d - jnp.where(at == 0, before, fallen(step - 1, n, k))
+                done[step, n, k] = (f + (d + (r - pltpu.roll(r, 1, 1)))) * kept[k]
+            return done[step, n, k]
+
+        def raised(step, n, k):
+            return once(("up", step, n, k), lambda: pltpu.roll(field(step, n, k), EDGE - 1, 0))
+
+        def fallen(step, n, k):
+            return once(("down", step, n, k), lambda: pltpu.roll(flux(step, k)[n][0], 1, 0))
+
+        def flux(step, k):
+            def make():
+                down, right = [], []
+                for n in range(2):
+                    f = field(step, n, k)
+                    below = raised(step, n, min(k + 1, count - 1))
+                    down.append(jnp.where(at == EDGE - 1, below, raised(step, n, k)) - f)
+                    right.append(pltpu.roll(f, PROBE - 1, 1) - f)
+                square = down[0] * down[0] + right[0] * right[0] + (down[1] * down[1] + right[1] * right[1])
+                gain = weights[k] * lax.rsqrt(square + TV_EPS)
+                return [(gain * d, gain * r) for d, r in zip(down, right)]
+            return once(("flux", step, k), make)
+
+        for k in range(1, count - 1):
+            for n in range(2):
+                out[2 * s + n, EDGE * (k - 1) : EDGE * k] = field(TV_STEPS, n, k)[:, :CORE]
 
     put(2, wr * gr_ + wi * gi_)
     put(3, wr * gi_ - wi * gr_)

time: 30.5 us -> 30.4 us (level)
  no operation moved by 1% of the time
where the time goes in v7:
time: 30.4 us; the launch traced here: 29.9 us
  Pallas kernels  29.2 us (96%)
  local copies, waits for them, and re-layouts  0.71 us (2%)
    pallas_call x1, Pallas kernels, body(): pl.pallas_call(whole_kernel, out_shape=pltpu.VMEM((4, CORE, CORE), F32),...  29.2 us
    unnamed x1, local copies, waits for them, and re-layouts  0.71 us

profile of v7, /device:TPU:1, one launch (start us, length us, event | category | flops | bytes accessed | tf_op | source)
XLA Modules:
  0.0 29.9 jit_solution(4029990893237557323)
XLA Ops:
  0.0 29.2 %ptycho.1 = f32[4,128,128]{2,1,0:T(8,128)S(1)} custom-call(s32[2]{0:T(128)} %bitcast.7, f32[4,128,128]{2,1,0:T(8,128)} %bitcast.5, f32[128,128]{1,0:T(8,128)} %w_any.1, f32[2,256,256]{2,1,0:T(8,128)} %probe_any.1, f32[256,256]{1,0:T(8,128)} %phase_any.1, f32[256,256]{1,0:T(8,128)} %bitcast.6, bf16[10,256,256]{2,1,0:T(8,128)(2,1)} %constant.2.clone.tab_any), custom_call_target="tpu_custom_call" | custom-call | tf_op jit(solution)/shard_map/ptycho/pallas_call | solution.py:633
  29.2 0.7 %copy.9 = f32[2,2,128,128]{3,2,1,0:T(8,128)} copy(f32[2,2,128,128]{3,2,1,0:T(8,128)S(1)} %bitcast.4) | data formatting | bytes 524288
